TPU v7x, 512 devices: a whole 4x4x16 slice. The times are simulated.
512 devices in a mesh: seq: 16 (over z), head: 32 (over x, y, core).
Axes of the slice: x: 4, y: 4, z: 16, core: 2. Of those that a mesh axis runs over, the one named last changes fastest.
Arguments:
- queries: bfloat16 [16384, 8192], P('seq', 'head'), may hold values from -6 to 6
- keys: bfloat16 [16384, 8192], P('seq', 'head'), may hold values from -1 to 1
- values: bfloat16 [16384, 8192], P('seq', 'head'), may hold values from -40 to 40
- log_decay: float32 [64, 16384], P('head', 'seq'), may hold values from -1 to 0
- gain: float32 [8192], P('head'), may hold values from 0.25 to 1.75
- out_grad: bfloat16 [16384, 8192], P('seq', 'head'), may hold values from -16 to 16
Outputs:
- output: bfloat16 [16384, 8192], P('seq', 'head')
- query_grad: bfloat16 [16384, 8192], P('seq', 'head')
- key_grad: bfloat16 [16384, 8192], P('seq', 'head')
- value_grad: bfloat16 [16384, 8192], P('seq', 'head')
- gain_grad: float32 [8192], P('head')
All inputs are finite; a program needn't handle non-finite values.
Results may differ from a plain program's by a relative error of at most 0.001.
Values sent between devices are 32-bit elements; how exact they have to be, the bound alone decides.
No kernel may reach another device: no remote copies, remote signals or barrier semaphores. Data moves between devices by JAX's collectives and lax.ppermute only.
A program may use at most 64 MiB of HBM per device.

v0:
```python
import jax
import jax.numpy as jnp
from jax import lax
from jax.sharding import PartitionSpec as P

epsilon = 1e-06
highest = lax.Precision.HIGHEST


def passed_along(value, axis, steps):
    count = lax.axis_size(axis)
    initial, last = (max(0, -steps), min(count, count - steps))
    return lax.ppermute(value, axis, [(source, source + steps) for source in range(initial, last)])


def to_blocks(matrix, heads_local, block_count, block_rows):
    head_width = matrix.shape[1] // heads_local
    return matrix.reshape(block_count, block_rows, heads_local, head_width).transpose(2, 0, 1, 3)


def from_blocks(blocked):
    heads_local, block_count, block_rows, head_width = blocked.shape
    return blocked.transpose(1, 2, 0, 3).reshape(block_count * block_rows, heads_local * head_width)


def carry_forward(device_decay, device_state):

    def relay_step(iteration, prefix):
        outgoing = jnp.exp(device_decay)[:, None, None] * prefix + device_state
        return passed_along(outgoing, "seq", 1)

    return lax.fori_loop(0, lax.axis_size("seq") - 1, relay_step, jnp.zeros_like(device_state))


def carry_backward(device_decay, device_back):

    def relay_step(iteration, suffix):
        outgoing = jnp.exp(device_decay)[:, None, None] * suffix + device_back
        return passed_along(outgoing, "seq", -1)

    return lax.fori_loop(0, lax.axis_size("seq") - 1, relay_step, jnp.zeros_like(device_back))


def local(queries, keys, values, log_decay, gain, out_grad):
    token_rows, channels = queries.shape
    heads_local = log_decay.shape[0]
    block_rows = min(256, token_rows)
    block_count = token_rows // block_rows
    total_channels = channels * lax.axis_size("head")
    query_narrow = to_blocks(queries, heads_local, block_count, block_rows)
    key_narrow = to_blocks(keys, heads_local, block_count, block_rows)
    query_blocks = query_narrow.astype(jnp.float32)
    key_blocks = key_narrow.astype(jnp.float32)
    value_blocks = to_blocks(values, heads_local, block_count, block_rows).astype(jnp.float32)
    decay_sum = jnp.cumsum(log_decay.reshape(heads_local, block_count, block_rows), axis=2)
    block_total = decay_sum[:, :, -1]
    causal = jnp.arange(block_rows)[:, None] >= jnp.arange(block_rows)[None, :]
    mask_decay = jnp.exp(
        jnp.where(causal, decay_sum[..., :, None] - decay_sum[..., None, :], -1e30)
    )
    from_start = jnp.exp(decay_sum)[..., None]
    to_end = jnp.exp(block_total[..., None] - decay_sum)[..., None]
    scores = (
        jnp.einsum("hnid,hnjd->hnij", query_narrow, key_narrow, preferred_element_type=jnp.float32)
        * mask_decay
    )
    inside = jnp.einsum("hnij,hnjd->hnid", scores, value_blocks, precision=highest)
    own_states = jnp.einsum("hnjd,hnje->hnde", key_blocks * to_end, value_blocks, precision=highest)
    device_decay = jnp.sum(block_total, axis=1)
    device_state = jnp.zeros_like(own_states[:, 0])
    for block_index in range(block_count):
        device_state = (
            jnp.exp(block_total[:, block_index])[:, None, None] * device_state
            + own_states[:, block_index]
        )
    incoming = carry_forward(device_decay, device_state)
    entering = []
    running = incoming
    for block_index in range(block_count):
        entering.append(running)
        running = (
            jnp.exp(block_total[:, block_index])[:, None, None] * running
            + own_states[:, block_index]
        )
    entering = jnp.stack(entering, axis=1)
    attended = inside + from_start * jnp.einsum(
        "hnid,hnde->hnie", query_blocks, entering, precision=highest
    )
    flattened = from_blocks(attended)
    grad_wide = out_grad.astype(jnp.float32)
    normed_grad = grad_wide * gain
    squares = lax.psum(jnp.sum(flattened * flattened, axis=1), "head")
    inverse = 1.0 / jnp.sqrt(squares / total_channels + epsilon)
    normed = flattened * inverse[:, None]
    projected = lax.psum(jnp.sum(normed_grad * normed, axis=1), "head")
    output = (normed * gain).astype(jnp.bfloat16)
    gain_part = jnp.sum(grad_wide * normed, axis=0)
    flat_grad = (normed_grad - normed * (projected / total_channels)[:, None]) * inverse[:, None]
    attended_grad = to_blocks(flat_grad, heads_local, block_count, block_rows)
    score_grad = (
        jnp.einsum("hnid,hnjd->hnij", attended_grad, value_blocks, precision=highest) * mask_decay
    )
    query_grad = jnp.einsum("hnij,hnjd->hnid", score_grad, key_blocks, precision=highest)
    query_grad = query_grad + from_start * jnp.einsum(
        "hnie,hnde->hnid", attended_grad, entering, precision=highest
    )
    key_grad = jnp.einsum("hnij,hnid->hnjd", score_grad, query_blocks, precision=highest)
    value_grad = jnp.einsum("hnij,hnid->hnjd", scores, attended_grad, precision=highest)
    own_back = jnp.einsum(
        "hnid,hnie->hnde", query_blocks * from_start, attended_grad, precision=highest
    )
    device_back = jnp.zeros_like(device_state)
    for block_index in reversed(range(block_count)):
        device_back = (
            own_back[:, block_index]
            + jnp.exp(block_total[:, block_index])[:, None, None] * device_back
        )
    later_sum = carry_backward(device_decay, device_back)
    leaving = []
    running = later_sum
    for block_index in reversed(range(block_count)):
        leaving.append(running)
        running = (
            own_back[:, block_index] + jnp.exp(block_total[:, block_index])[:, None, None] * running
        )
    leaving = jnp.stack(leaving[::-1], axis=1)
    key_grad = key_grad + to_end * jnp.einsum(
        "hnje,hnde->hnjd", value_blocks, leaving, precision=highest
    )
    value_grad = value_grad + to_end * jnp.einsum(
        "hnjd,hnde->hnje", key_blocks, leaving, precision=highest
    )
    gain_grad = lax.psum(gain_part, "seq")
    return (
        output,
        from_blocks(query_grad).astype(jnp.bfloat16),
        from_blocks(key_grad).astype(jnp.bfloat16),
        from_blocks(value_grad).astype(jnp.bfloat16),
        gain_grad,
    )


def solution(mesh):
    in_specs = (
        P("seq", "head"),
        P("seq", "head"),
        P("seq", "head"),
        P("head", "seq"),
        P("head"),
        P("seq", "head"),
    )
    out_specs = (P("seq", "head"), P("seq", "head"), P("seq", "head"), P("seq", "head"), P("head"))
    return jax.shard_map(local, mesh=mesh, in_specs=in_specs, out_specs=out_specs, check_vma=False)
```

profile of v0, /device:TPU:96, one launch (start us, length us, event | category | flops | bytes accessed | tf_op | source)
XLA Modules:
  0.0 471.4 jit_solution(15646903390274113141)
XLA Ops:
  9.9 125.4 %while.24 = (s32[]{:T(128)}, f32[2,128,128]{2,1,0:T(8,128)S(1)}, f32[2,1,1]{0,2,1:T(1,128)S(1)}, f32[2,128,128]{2,1,0:T(8,128)S(1)}, s32[]{:T(128)}) while((s32[]{:T(128)}, f32[2,128,128]{2,1,0:T(8,128)S(1)}, f32[2,1,1]{0,2,1:T(1,128)S(1)}, f32[2,128,128]{2,1,0:T(8,128)S(1)}, s32[]{:T(128)}) %tuple.63), condition=%wide.region_4.5_spmd, body=%wide.region_3.4_spmd.sunk | while | flops 65538 | bytes 917613 | solution.py:32
  17.8 5.6 %collective-permute-start = (f32[2,128,128]{2,1,0:T(8,128)S(1)}, f32[2,128,128]{2,1,0:T(8,128)S(1)}, u32[]{:S(2)}, u32[]{:S(2)}) collective-permute-start(f32[2,128,128]{2,1,0:T(8,128)S(1)} %multiply_add_fusion.10), channel_id=1, source_target_pairs={{0,32},{32,64},{64,96},{96,128},{128,160},{160,192},{192,224},{224... | collective-permute-start | bytes 393224 | tf_op jit(solution)/shard_map/while/body/eval_jaxpr/ppermute | solution.py:13
  26.0 5.6 %collective-permute-start = (f32[2,128,128]{2,1,0:T(8,128)S(1)}, f32[2,128,128]{2,1,0:T(8,128)S(1)}, u32[]{:S(2)}, u32[]{:S(2)}) collective-permute-start(f32[2,128,128]{2,1,0:T(8,128)S(1)} %multiply_add_fusion.10), channel_id=1, source_target_pairs={{0,32},{32,64},{64,96},{96,128},{128,160},{160,192},{192,224},{224... | collective-permute-start | bytes 393224 | tf_op jit(solution)/shard_map/while/body/eval_jaxpr/ppermute | solution.py:13
  34.2 5.6 %collective-permute-start = (f32[2,128,128]{2,1,0:T(8,128)S(1)}, f32[2,128,128]{2,1,0:T(8,128)S(1)}, u32[]{:S(2)}, u32[]{:S(2)}) collective-permute-start(f32[2,128,128]{2,1,0:T(8,128)S(1)} %multiply_add_fusion.10), channel_id=1, source_target_pairs={{0,32},{32,64},{64,96},{96,128},{128,160},{160,192},{192,224},{224... | collective-permute-start | bytes 393224 | tf_op jit(solution)/shard_map/while/body/eval_jaxpr/ppermute | solution.py:13
  42.3 5.6 %collective-permute-start = (f32[2,128,128]{2,1,0:T(8,128)S(1)}, f32[2,128,128]{2,1,0:T(8,128)S(1)}, u32[]{:S(2)}, u32[]{:S(2)}) collective-permute-start(f32[2,128,128]{2,1,0:T(8,128)S(1)} %multiply_add_fusion.10), channel_id=1, source_target_pairs={{0,32},{32,64},{64,96},{96,128},{128,160},{160,192},{192,224},{224... | collective-permute-start | bytes 393224 | tf_op jit(solution)/shard_map/while/body/eval_jaxpr/ppermute | solution.py:13
  50.5 5.6 %collective-permute-start = (f32[2,128,128]{2,1,0:T(8,128)S(1)}, f32[2,128,128]{2,1,0:T(8,128)S(1)}, u32[]{:S(2)}, u32[]{:S(2)}) collective-permute-start(f32[2,128,128]{2,1,0:T(8,128)S(1)} %multiply_add_fusion.10), channel_id=1, source_target_pairs={{0,32},{32,64},{64,96},{96,128},{128,160},{160,192},{192,224},{224... | collective-permute-start | bytes 393224 | tf_op jit(solution)/shard_map/while/body/eval_jaxpr/ppermute | solution.py:13
  59.6 5.6 %collective-permute-start = (f32[2,128,128]{2,1,0:T(8,128)S(1)}, f32[2,128,128]{2,1,0:T(8,128)S(1)}, u32[]{:S(2)}, u32[]{:S(2)}) collective-permute-start(f32[2,128,128]{2,1,0:T(8,128)S(1)} %multiply_add_fusion.10), channel_id=1, source_target_pairs={{0,32},{32,64},{64,96},{96,128},{128,160},{160,192},{192,224},{224... | collective-permute-start | bytes 393224 | tf_op jit(solution)/shard_map/while/body/eval_jaxpr/ppermute | solution.py:13
  68.4 5.6 %collective-permute-start = (f32[2,128,128]{2,1,0:T(8,128)S(1)}, f32[2,128,128]{2,1,0:T(8,128)S(1)}, u32[]{:S(2)}, u32[]{:S(2)}) collective-permute-start(f32[2,128,128]{2,1,0:T(8,128)S(1)} %multiply_add_fusion.10), channel_id=1, source_target_pairs={{0,32},{32,64},{64,96},{96,128},{128,160},{160,192},{192,224},{224... | collective-permute-start | bytes 393224 | tf_op jit(solution)/shard_map/while/body/eval_jaxpr/ppermute | solution.py:13
  76.6 5.6 %collective-permute-start = (f32[2,128,128]{2,1,0:T(8,128)S(1)}, f32[2,128,128]{2,1,0:T(8,128)S(1)}, u32[]{:S(2)}, u32[]{:S(2)}) collective-permute-start(f32[2,128,128]{2,1,0:T(8,128)S(1)} %multiply_add_fusion.10), channel_id=1, source_target_pairs={{0,32},{32,64},{64,96},{96,128},{128,160},{160,192},{192,224},{224... | collective-permute-start | bytes 393224 | tf_op jit(solution)/shard_map/while/body/eval_jaxpr/ppermute | solution.py:13
  92.9 5.6 %collective-permute-start = (f32[2,128,128]{2,1,0:T(8,128)S(1)}, f32[2,128,128]{2,1,0:T(8,128)S(1)}, u32[]{:S(2)}, u32[]{:S(2)}) collective-permute-start(f32[2,128,128]{2,1,0:T(8,128)S(1)} %multiply_add_fusion.10), channel_id=1, source_target_pairs={{0,32},{32,64},{64,96},{96,128},{128,160},{160,192},{192,224},{224... | collective-permute-start | bytes 393224 | tf_op jit(solution)/shard_map/while/body/eval_jaxpr/ppermute | solution.py:13
  109.8 5.6 %collective-permute-start = (f32[2,128,128]{2,1,0:T(8,128)S(1)}, f32[2,128,128]{2,1,0:T(8,128)S(1)}, u32[]{:S(2)}, u32[]{:S(2)}) collective-permute-start(f32[2,128,128]{2,1,0:T(8,128)S(1)} %multiply_add_fusion.10), channel_id=1, source_target_pairs={{0,32},{32,64},{64,96},{96,128},{128,160},{160,192},{192,224},{224... | collective-permute-start | bytes 393224 | tf_op jit(solution)/shard_map/while/body/eval_jaxpr/ppermute | solution.py:13
  119.0 5.6 %collective-permute-start = (f32[2,128,128]{2,1,0:T(8,128)S(1)}, f32[2,128,128]{2,1,0:T(8,128)S(1)}, u32[]{:S(2)}, u32[]{:S(2)}) collective-permute-start(f32[2,128,128]{2,1,0:T(8,128)S(1)} %multiply_add_fusion.10), channel_id=1, source_target_pairs={{0,32},{32,64},{64,96},{96,128},{128,160},{160,192},{192,224},{224... | collective-permute-start | bytes 393224 | tf_op jit(solution)/shard_map/while/body/eval_jaxpr/ppermute | solution.py:13
  139.9 62.7 %psum.21 = f32[1024]{0:T(1024)S(1)} all-reduce(f32[1024]{0:T(1024)S(1)} %bitcast.231), channel_id=1, replica_groups=mesh['seq'=16,'head'=32] {'head'}, use_global_device_ids=true, to_apply=%region_6.7 | all-reduce | flops 1024 | bytes 8192 | tf_op jit(solution)/shard_map/psum | solution.py:92
  204.7 32.4 %psum.23 = f32[256]{0:T(256)} all-reduce(f32[256]{0:T(256)S(1)} %get-tuple-element.107), channel_id=1, replica_groups=mesh['seq'=16,'head'=32] {'seq'}, use_global_device_ids=true, to_apply=%region_12.13 | all-reduce | flops 256 | bytes 2048 | tf_op jit(solution)/shard_map/psum | solution.py:133
  237.2 62.7 %psum.22 = f32[1024]{0:T(1024)S(1)} all-reduce(f32[1024]{0:T(1024)S(1)} %get-tuple-element.108), channel_id=1, replica_groups=mesh['seq'=16,'head'=32] {'head'}, use_global_device_ids=true, to_apply=%region_8.9 | all-reduce | flops 1024 | bytes 8192 | tf_op jit(solution)/shard_map/psum | solution.py:95
  303.1 6.1 %convolution_bitcast_fusion.4 = f32[4,256,2,128]{3,1,0,2:T(8,128)} fusion(f32[2,4,256,256]{3,2,1,0:T(8,128)} %copy-done, f32[4,256,2,128]{3,2,1,0:T(2,128)S(1)} %reshape.129), kind=kOutput, calls=%fused_computation.11 | convolution fusion | flops 805306368 | bytes 4194304 | tf_op jit(solution)/shard_map/hnij,hnid->hnjd/dot_general | solution.py:108
  310.5 147.5 %while.25 = (s32[]{:T(128)}, f32[2,128,128]{2,1,0:T(8,128)S(1)}, f32[2,1,1]{0,2,1:T(1,128)}, f32[2,128,128]{2,1,0:T(8,128)S(1)}, s32[]{:T(128)}) while((s32[]{:T(128)}, f32[2,128,128]{2,1,0:T(8,128)S(1)}, f32[2,1,1]{0,2,1:T(1,128)}, f32[2,128,128]{2,1,0:T(8,128)S(1)}, s32[]{:T(128)}) %tuple.69), condition=%wide.region_10.11_spmd, body=%wide.region_9.10_spmd.sunk | while | flops 65538 | bytes 917613 | solution.py:41
  314.1 6.6 %collective-permute-done.1 = f32[2,128,128]{2,1,0:T(8,128)S(1)} collective-permute-done((f32[2,128,128]{2,1,0:T(8,128)}, f32[2,128,128]{2,1,0:T(8,128)S(1)}, u32[]{:S(2)}, u32[]{:S(2)}) %collective-permute-start.1) | collective-permute-done | bytes 131104 | tf_op jit(solution)/shard_map/while/body/eval_jaxpr/ppermute | solution.py:13
  324.0 6.4 %collective-permute-done.1 = f32[2,128,128]{2,1,0:T(8,128)S(1)} collective-permute-done((f32[2,128,128]{2,1,0:T(8,128)}, f32[2,128,128]{2,1,0:T(8,128)S(1)}, u32[]{:S(2)}, u32[]{:S(2)}) %collective-permute-start.1) | collective-permute-done | bytes 131104 | tf_op jit(solution)/shard_map/while/body/eval_jaxpr/ppermute | solution.py:13
  333.7 6.4 %collective-permute-done.1 = f32[2,128,128]{2,1,0:T(8,128)S(1)} collective-permute-done((f32[2,128,128]{2,1,0:T(8,128)}, f32[2,128,128]{2,1,0:T(8,128)S(1)}, u32[]{:S(2)}, u32[]{:S(2)}) %collective-permute-start.1) | collective-permute-done | bytes 131104 | tf_op jit(solution)/shard_map/while/body/eval_jaxpr/ppermute | solution.py:13
  343.4 6.4 %collective-permute-done.1 = f32[2,128,128]{2,1,0:T(8,128)S(1)} collective-permute-done((f32[2,128,128]{2,1,0:T(8,128)}, f32[2,128,128]{2,1,0:T(8,128)S(1)}, u32[]{:S(2)}, u32[]{:S(2)}) %collective-permute-start.1) | collective-permute-done | bytes 131104 | tf_op jit(solution)/shard_map/while/body/eval_jaxpr/ppermute | solution.py:13
  353.1 6.4 %collective-permute-done.1 = f32[2,128,128]{2,1,0:T(8,128)S(1)} collective-permute-done((f32[2,128,128]{2,1,0:T(8,128)}, f32[2,128,128]{2,1,0:T(8,128)S(1)}, u32[]{:S(2)}, u32[]{:S(2)}) %collective-permute-start.1) | collective-permute-done | bytes 131104 | tf_op jit(solution)/shard_map/while/body/eval_jaxpr/ppermute | solution.py:13
  362.8 6.4 %collective-permute-done.1 = f32[2,128,128]{2,1,0:T(8,128)S(1)} collective-permute-done((f32[2,128,128]{2,1,0:T(8,128)}, f32[2,128,128]{2,1,0:T(8,128)S(1)}, u32[]{:S(2)}, u32[]{:S(2)}) %collective-permute-start.1) | collective-permute-done | bytes 131104 | tf_op jit(solution)/shard_map/while/body/eval_jaxpr/ppermute | solution.py:13
  372.4 6.9 %collective-permute-done.1 = f32[2,128,128]{2,1,0:T(8,128)S(1)} collective-permute-done((f32[2,128,128]{2,1,0:T(8,128)}, f32[2,128,128]{2,1,0:T(8,128)S(1)}, u32[]{:S(2)}, u32[]{:S(2)}) %collective-permute-start.1) | collective-permute-done | bytes 131104 | tf_op jit(solution)/shard_map/while/body/eval_jaxpr/ppermute | solution.py:13
  382.7 7.4 %collective-permute-done.1 = f32[2,128,128]{2,1,0:T(8,128)S(1)} collective-permute-done((f32[2,128,128]{2,1,0:T(8,128)}, f32[2,128,128]{2,1,0:T(8,128)S(1)}, u32[]{:S(2)}, u32[]{:S(2)}) %collective-permute-start.1) | collective-permute-done | bytes 131104 | tf_op jit(solution)/shard_map/while/body/eval_jaxpr/ppermute | solution.py:13
  393.4 6.6 %collective-permute-done.1 = f32[2,128,128]{2,1,0:T(8,128)S(1)} collective-permute-done((f32[2,128,128]{2,1,0:T(8,128)}, f32[2,128,128]{2,1,0:T(8,128)S(1)}, u32[]{:S(2)}, u32[]{:S(2)}) %collective-permute-start.1) | collective-permute-done | bytes 131104 | tf_op jit(solution)/shard_map/while/body/eval_jaxpr/ppermute | solution.py:13
  403.3 6.4 %collective-permute-done.1 = f32[2,128,128]{2,1,0:T(8,128)S(1)} collective-permute-done((f32[2,128,128]{2,1,0:T(8,128)}, f32[2,128,128]{2,1,0:T(8,128)S(1)}, u32[]{:S(2)}, u32[]{:S(2)}) %collective-permute-start.1) | collective-permute-done | bytes 131104 | tf_op jit(solution)/shard_map/while/body/eval_jaxpr/ppermute | solution.py:13
  413.0 6.4 %collective-permute-done.1 = f32[2,128,128]{2,1,0:T(8,128)S(1)} collective-permute-done((f32[2,128,128]{2,1,0:T(8,128)}, f32[2,128,128]{2,1,0:T(8,128)S(1)}, u32[]{:S(2)}, u32[]{:S(2)}) %collective-permute-start.1) | collective-permute-done | bytes 131104 | tf_op jit(solution)/shard_map/while/body/eval_jaxpr/ppermute | solution.py:13
  422.7 6.4 %collective-permute-done.1 = f32[2,128,128]{2,1,0:T(8,128)S(1)} collective-permute-done((f32[2,128,128]{2,1,0:T(8,128)}, f32[2,128,128]{2,1,0:T(8,128)S(1)}, u32[]{:S(2)}, u32[]{:S(2)}) %collective-permute-start.1) | collective-permute-done | bytes 131104 | tf_op jit(solution)/shard_map/while/body/eval_jaxpr/ppermute | solution.py:13
  432.4 6.4 %collective-permute-done.1 = f32[2,128,128]{2,1,0:T(8,128)S(1)} collective-permute-done((f32[2,128,128]{2,1,0:T(8,128)}, f32[2,128,128]{2,1,0:T(8,128)S(1)}, u32[]{:S(2)}, u32[]{:S(2)}) %collective-permute-start.1) | collective-permute-done | bytes 131104 | tf_op jit(solution)/shard_map/while/body/eval_jaxpr/ppermute | solution.py:13
  442.1 6.4 %collective-permute-done.1 = f32[2,128,128]{2,1,0:T(8,128)S(1)} collective-permute-done((f32[2,128,128]{2,1,0:T(8,128)}, f32[2,128,128]{2,1,0:T(8,128)S(1)}, u32[]{:S(2)}, u32[]{:S(2)}) %collective-permute-start.1) | collective-permute-done | bytes 131104 | tf_op jit(solution)/shard_map/while/body/eval_jaxpr/ppermute | solution.py:13
  451.7 6.4 %collective-permute-done.1 = f32[2,128,128]{2,1,0:T(8,128)S(1)} collective-permute-done((f32[2,128,128]{2,1,0:T(8,128)}, f32[2,128,128]{2,1,0:T(8,128)S(1)}, u32[]{:S(2)}, u32[]{:S(2)}) %collective-permute-start.1) | collective-permute-done | bytes 131104 | tf_op jit(solution)/shard_map/while/body/eval_jaxpr/ppermute | solution.py:13
  (162 shorter events, 147.0 us)
Async XLA Ops:
  4.7 130.6 %copy-start.15 = (f32[2]{0:T(128)}, f32[2]{0:T(128)S(1)}, u32[]{:S(2)}) copy-start(f32[2]{0:T(128)S(1)} %get-tuple-element.111) | copy-start | bytes 28
  4.7 130.6 %copy-start.17 = (f32[2]{0:T(128)}, f32[2]{0:T(128)S(1)}, u32[]{:S(2)}) copy-start(f32[2]{0:T(128)S(1)} %get-tuple-element.112) | copy-start | bytes 28
  10.0 7.8 %collective-permute-start = (f32[2,128,128]{2,1,0:T(8,128)S(1)}, f32[2,128,128]{2,1,0:T(8,128)S(1)}, u32[]{:S(2)}, u32[]{:S(2)}) collective-permute-start(f32[2,128,128]{2,1,0:T(8,128)S(1)} %multiply_add_fusion.10), channel_id=1, source_target_pairs={{0,32},{32,64},{64,96},{96,128},{128,160},{160,192},{192,224},{224... | collective-permute-start | bytes 393224 | tf_op jit(solution)/shard_map/while/body/eval_jaxpr/ppermute | solution.py:13
  17.8 8.1 %collective-permute-start = (f32[2,128,128]{2,1,0:T(8,128)S(1)}, f32[2,128,128]{2,1,0:T(8,128)S(1)}, u32[]{:S(2)}, u32[]{:S(2)}) collective-permute-start(f32[2,128,128]{2,1,0:T(8,128)S(1)} %multiply_add_fusion.10), channel_id=1, source_target_pairs={{0,32},{32,64},{64,96},{96,128},{128,160},{160,192},{192,224},{224... | collective-permute-start | bytes 393224 | tf_op jit(solution)/shard_map/while/body/eval_jaxpr/ppermute | solution.py:13
  26.0 8.1 %collective-permute-start = (f32[2,128,128]{2,1,0:T(8,128)S(1)}, f32[2,128,128]{2,1,0:T(8,128)S(1)}, u32[]{:S(2)}, u32[]{:S(2)}) collective-permute-start(f32[2,128,128]{2,1,0:T(8,128)S(1)} %multiply_add_fusion.10), channel_id=1, source_target_pairs={{0,32},{32,64},{64,96},{96,128},{128,160},{160,192},{192,224},{224... | collective-permute-start | bytes 393224 | tf_op jit(solution)/shard_map/while/body/eval_jaxpr/ppermute | solution.py:13
  34.2 8.1 %collective-permute-start = (f32[2,128,128]{2,1,0:T(8,128)S(1)}, f32[2,128,128]{2,1,0:T(8,128)S(1)}, u32[]{:S(2)}, u32[]{:S(2)}) collective-permute-start(f32[2,128,128]{2,1,0:T(8,128)S(1)} %multiply_add_fusion.10), channel_id=1, source_target_pairs={{0,32},{32,64},{64,96},{96,128},{128,160},{160,192},{192,224},{224... | collective-permute-start | bytes 393224 | tf_op jit(solution)/shard_map/while/body/eval_jaxpr/ppermute | solution.py:13
  42.3 8.1 %collective-permute-start = (f32[2,128,128]{2,1,0:T(8,128)S(1)}, f32[2,128,128]{2,1,0:T(8,128)S(1)}, u32[]{:S(2)}, u32[]{:S(2)}) collective-permute-start(f32[2,128,128]{2,1,0:T(8,128)S(1)} %multiply_add_fusion.10), channel_id=1, source_target_pairs={{0,32},{32,64},{64,96},{96,128},{128,160},{160,192},{192,224},{224... | collective-permute-start | bytes 393224 | tf_op jit(solution)/shard_map/while/body/eval_jaxpr/ppermute | solution.py:13
  50.5 9.0 %collective-permute-start = (f32[2,128,128]{2,1,0:T(8,128)S(1)}, f32[2,128,128]{2,1,0:T(8,128)S(1)}, u32[]{:S(2)}, u32[]{:S(2)}) collective-permute-start(f32[2,128,128]{2,1,0:T(8,128)S(1)} %multiply_add_fusion.10), channel_id=1, source_target_pairs={{0,32},{32,64},{64,96},{96,128},{128,160},{160,192},{192,224},{224... | collective-permute-start | bytes 393224 | tf_op jit(solution)/shard_map/while/body/eval_jaxpr/ppermute | solution.py:13
  59.6 8.7 %collective-permute-start = (f32[2,128,128]{2,1,0:T(8,128)S(1)}, f32[2,128,128]{2,1,0:T(8,128)S(1)}, u32[]{:S(2)}, u32[]{:S(2)}) collective-permute-start(f32[2,128,128]{2,1,0:T(8,128)S(1)} %multiply_add_fusion.10), channel_id=1, source_target_pairs={{0,32},{32,64},{64,96},{96,128},{128,160},{160,192},{192,224},{224... | collective-permute-start | bytes 393224 | tf_op jit(solution)/shard_map/while/body/eval_jaxpr/ppermute | solution.py:13
  68.4 8.1 %collective-permute-start = (f32[2,128,128]{2,1,0:T(8,128)S(1)}, f32[2,128,128]{2,1,0:T(8,128)S(1)}, u32[]{:S(2)}, u32[]{:S(2)}) collective-permute-start(f32[2,128,128]{2,1,0:T(8,128)S(1)} %multiply_add_fusion.10), channel_id=1, source_target_pairs={{0,32},{32,64},{64,96},{96,128},{128,160},{160,192},{192,224},{224... | collective-permute-start | bytes 393224 | tf_op jit(solution)/shard_map/while/body/eval_jaxpr/ppermute | solution.py:13
  76.6 8.1 %collective-permute-start = (f32[2,128,128]{2,1,0:T(8,128)S(1)}, f32[2,128,128]{2,1,0:T(8,128)S(1)}, u32[]{:S(2)}, u32[]{:S(2)}) collective-permute-start(f32[2,128,128]{2,1,0:T(8,128)S(1)} %multiply_add_fusion.10), channel_id=1, source_target_pairs={{0,32},{32,64},{64,96},{96,128},{128,160},{160,192},{192,224},{224... | collective-permute-start | bytes 393224 | tf_op jit(solution)/shard_map/while/body/eval_jaxpr/ppermute | solution.py:13
  84.8 8.1 %collective-permute-start = (f32[2,128,128]{2,1,0:T(8,128)S(1)}, f32[2,128,128]{2,1,0:T(8,128)S(1)}, u32[]{:S(2)}, u32[]{:S(2)}) collective-permute-start(f32[2,128,128]{2,1,0:T(8,128)S(1)} %multiply_add_fusion.10), channel_id=1, source_target_pairs={{0,32},{32,64},{64,96},{96,128},{128,160},{160,192},{192,224},{224... | collective-permute-start | bytes 393224 | tf_op jit(solution)/shard_map/while/body/eval_jaxpr/ppermute | solution.py:13
  92.9 8.1 %collective-permute-start = (f32[2,128,128]{2,1,0:T(8,128)S(1)}, f32[2,128,128]{2,1,0:T(8,128)S(1)}, u32[]{:S(2)}, u32[]{:S(2)}) collective-permute-start(f32[2,128,128]{2,1,0:T(8,128)S(1)} %multiply_add_fusion.10), channel_id=1, source_target_pairs={{0,32},{32,64},{64,96},{96,128},{128,160},{160,192},{192,224},{224... | collective-permute-start | bytes 393224 | tf_op jit(solution)/shard_map/while/body/eval_jaxpr/ppermute | solution.py:13
  101.1 8.6 %collective-permute-start = (f32[2,128,128]{2,1,0:T(8,128)S(1)}, f32[2,128,128]{2,1,0:T(8,128)S(1)}, u32[]{:S(2)}, u32[]{:S(2)}) collective-permute-start(f32[2,128,128]{2,1,0:T(8,128)S(1)} %multiply_add_fusion.10), channel_id=1, source_target_pairs={{0,32},{32,64},{64,96},{96,128},{128,160},{160,192},{192,224},{224... | collective-permute-start | bytes 393224 | tf_op jit(solution)/shard_map/while/body/eval_jaxpr/ppermute | solution.py:13
  109.8 9.2 %collective-permute-start = (f32[2,128,128]{2,1,0:T(8,128)S(1)}, f32[2,128,128]{2,1,0:T(8,128)S(1)}, u32[]{:S(2)}, u32[]{:S(2)}) collective-permute-start(f32[2,128,128]{2,1,0:T(8,128)S(1)} %multiply_add_fusion.10), channel_id=1, source_target_pairs={{0,32},{32,64},{64,96},{96,128},{128,160},{160,192},{192,224},{224... | collective-permute-start | bytes 393224 | tf_op jit(solution)/shard_map/while/body/eval_jaxpr/ppermute | solution.py:13
  119.0 8.1 %collective-permute-start = (f32[2,128,128]{2,1,0:T(8,128)S(1)}, f32[2,128,128]{2,1,0:T(8,128)S(1)}, u32[]{:S(2)}, u32[]{:S(2)}) collective-permute-start(f32[2,128,128]{2,1,0:T(8,128)S(1)} %multiply_add_fusion.10), channel_id=1, source_target_pairs={{0,32},{32,64},{64,96},{96,128},{128,160},{160,192},{192,224},{224... | collective-permute-start | bytes 393224 | tf_op jit(solution)/shard_map/while/body/eval_jaxpr/ppermute | solution.py:13
  127.2 8.1 %collective-permute-start = (f32[2,128,128]{2,1,0:T(8,128)S(1)}, f32[2,128,128]{2,1,0:T(8,128)S(1)}, u32[]{:S(2)}, u32[]{:S(2)}) collective-permute-start(f32[2,128,128]{2,1,0:T(8,128)S(1)} %multiply_add_fusion.10), channel_id=1, source_target_pairs={{0,32},{32,64},{64,96},{96,128},{128,160},{160,192},{192,224},{224... | collective-permute-start | bytes 393224 | tf_op jit(solution)/shard_map/while/body/eval_jaxpr/ppermute | solution.py:13
  312.1 8.6 %collective-permute-start.1 = (f32[2,128,128]{2,1,0:T(8,128)}, f32[2,128,128]{2,1,0:T(8,128)S(1)}, u32[]{:S(2)}, u32[]{:S(2)}) collective-permute-start(f32[2,128,128]{2,1,0:T(8,128)} %multiply_add_fusion.11), channel_id=1, source_target_pairs={{32,0},{64,32},{96,64},{128,96},{160,128},{192,160},{224,192},{256... | collective-permute-start | bytes 393224 | tf_op jit(solution)/shard_map/while/body/eval_jaxpr/ppermute | solution.py:13
  322.1 8.3 %collective-permute-start.1 = (f32[2,128,128]{2,1,0:T(8,128)}, f32[2,128,128]{2,1,0:T(8,128)S(1)}, u32[]{:S(2)}, u32[]{:S(2)}) collective-permute-start(f32[2,128,128]{2,1,0:T(8,128)} %multiply_add_fusion.11), channel_id=1, source_target_pairs={{32,0},{64,32},{96,64},{128,96},{160,128},{192,160},{224,192},{256... | collective-permute-start | bytes 393224 | tf_op jit(solution)/shard_map/while/body/eval_jaxpr/ppermute | solution.py:13
  331.8 8.3 %collective-permute-start.1 = (f32[2,128,128]{2,1,0:T(8,128)}, f32[2,128,128]{2,1,0:T(8,128)S(1)}, u32[]{:S(2)}, u32[]{:S(2)}) collective-permute-start(f32[2,128,128]{2,1,0:T(8,128)} %multiply_add_fusion.11), channel_id=1, source_target_pairs={{32,0},{64,32},{96,64},{128,96},{160,128},{192,160},{224,192},{256... | collective-permute-start | bytes 393224 | tf_op jit(solution)/shard_map/while/body/eval_jaxpr/ppermute | solution.py:13
  341.5 8.3 %collective-permute-start.1 = (f32[2,128,128]{2,1,0:T(8,128)}, f32[2,128,128]{2,1,0:T(8,128)S(1)}, u32[]{:S(2)}, u32[]{:S(2)}) collective-permute-start(f32[2,128,128]{2,1,0:T(8,128)} %multiply_add_fusion.11), channel_id=1, source_target_pairs={{32,0},{64,32},{96,64},{128,96},{160,128},{192,160},{224,192},{256... | collective-permute-start | bytes 393224 | tf_op jit(solution)/shard_map/while/body/eval_jaxpr/ppermute | solution.py:13
  351.2 8.3 %collective-permute-start.1 = (f32[2,128,128]{2,1,0:T(8,128)}, f32[2,128,128]{2,1,0:T(8,128)S(1)}, u32[]{:S(2)}, u32[]{:S(2)}) collective-permute-start(f32[2,128,128]{2,1,0:T(8,128)} %multiply_add_fusion.11), channel_id=1, source_target_pairs={{32,0},{64,32},{96,64},{128,96},{160,128},{192,160},{224,192},{256... | collective-permute-start | bytes 393224 | tf_op jit(solution)/shard_map/while/body/eval_jaxpr/ppermute | solution.py:13
  360.8 8.3 %collective-permute-start.1 = (f32[2,128,128]{2,1,0:T(8,128)}, f32[2,128,128]{2,1,0:T(8,128)S(1)}, u32[]{:S(2)}, u32[]{:S(2)}) collective-permute-start(f32[2,128,128]{2,1,0:T(8,128)} %multiply_add_fusion.11), channel_id=1, source_target_pairs={{32,0},{64,32},{96,64},{128,96},{160,128},{192,160},{224,192},{256... | collective-permute-start | bytes 393224 | tf_op jit(solution)/shard_map/while/body/eval_jaxpr/ppermute | solution.py:13
  370.5 8.9 %collective-permute-start.1 = (f32[2,128,128]{2,1,0:T(8,128)}, f32[2,128,128]{2,1,0:T(8,128)S(1)}, u32[]{:S(2)}, u32[]{:S(2)}) collective-permute-start(f32[2,128,128]{2,1,0:T(8,128)} %multiply_add_fusion.11), channel_id=1, source_target_pairs={{32,0},{64,32},{96,64},{128,96},{160,128},{192,160},{224,192},{256... | collective-permute-start | bytes 393224 | tf_op jit(solution)/shard_map/while/body/eval_jaxpr/ppermute | solution.py:13
  380.8 9.3 %collective-permute-start.1 = (f32[2,128,128]{2,1,0:T(8,128)}, f32[2,128,128]{2,1,0:T(8,128)S(1)}, u32[]{:S(2)}, u32[]{:S(2)}) collective-permute-start(f32[2,128,128]{2,1,0:T(8,128)} %multiply_add_fusion.11), channel_id=1, source_target_pairs={{32,0},{64,32},{96,64},{128,96},{160,128},{192,160},{224,192},{256... | collective-permute-start | bytes 393224 | tf_op jit(solution)/shard_map/while/body/eval_jaxpr/ppermute | solution.py:13
  391.5 8.5 %collective-permute-start.1 = (f32[2,128,128]{2,1,0:T(8,128)}, f32[2,128,128]{2,1,0:T(8,128)S(1)}, u32[]{:S(2)}, u32[]{:S(2)}) collective-permute-start(f32[2,128,128]{2,1,0:T(8,128)} %multiply_add_fusion.11), channel_id=1, source_target_pairs={{32,0},{64,32},{96,64},{128,96},{160,128},{192,160},{224,192},{256... | collective-permute-start | bytes 393224 | tf_op jit(solution)/shard_map/while/body/eval_jaxpr/ppermute | solution.py:13
  401.4 8.3 %collective-permute-start.1 = (f32[2,128,128]{2,1,0:T(8,128)}, f32[2,128,128]{2,1,0:T(8,128)S(1)}, u32[]{:S(2)}, u32[]{:S(2)}) collective-permute-start(f32[2,128,128]{2,1,0:T(8,128)} %multiply_add_fusion.11), channel_id=1, source_target_pairs={{32,0},{64,32},{96,64},{128,96},{160,128},{192,160},{224,192},{256... | collective-permute-start | bytes 393224 | tf_op jit(solution)/shard_map/while/body/eval_jaxpr/ppermute | solution.py:13
  411.1 8.3 %collective-permute-start.1 = (f32[2,128,128]{2,1,0:T(8,128)}, f32[2,128,128]{2,1,0:T(8,128)S(1)}, u32[]{:S(2)}, u32[]{:S(2)}) collective-permute-start(f32[2,128,128]{2,1,0:T(8,128)} %multiply_add_fusion.11), channel_id=1, source_target_pairs={{32,0},{64,32},{96,64},{128,96},{160,128},{192,160},{224,192},{256... | collective-permute-start | bytes 393224 | tf_op jit(solution)/shard_map/while/body/eval_jaxpr/ppermute | solution.py:13
  420.8 8.3 %collective-permute-start.1 = (f32[2,128,128]{2,1,0:T(8,128)}, f32[2,128,128]{2,1,0:T(8,128)S(1)}, u32[]{:S(2)}, u32[]{:S(2)}) collective-permute-start(f32[2,128,128]{2,1,0:T(8,128)} %multiply_add_fusion.11), channel_id=1, source_target_pairs={{32,0},{64,32},{96,64},{128,96},{160,128},{192,160},{224,192},{256... | collective-permute-start | bytes 393224 | tf_op jit(solution)/shard_map/while/body/eval_jaxpr/ppermute | solution.py:13
  430.5 8.3 %collective-permute-start.1 = (f32[2,128,128]{2,1,0:T(8,128)}, f32[2,128,128]{2,1,0:T(8,128)S(1)}, u32[]{:S(2)}, u32[]{:S(2)}) collective-permute-start(f32[2,128,128]{2,1,0:T(8,128)} %multiply_add_fusion.11), channel_id=1, source_target_pairs={{32,0},{64,32},{96,64},{128,96},{160,128},{192,160},{224,192},{256... | collective-permute-start | bytes 393224 | tf_op jit(solution)/shard_map/while/body/eval_jaxpr/ppermute | solution.py:13
  440.1 8.3 %collective-permute-start.1 = (f32[2,128,128]{2,1,0:T(8,128)}, f32[2,128,128]{2,1,0:T(8,128)S(1)}, u32[]{:S(2)}, u32[]{:S(2)}) collective-permute-start(f32[2,128,128]{2,1,0:T(8,128)} %multiply_add_fusion.11), channel_id=1, source_target_pairs={{32,0},{64,32},{96,64},{128,96},{160,128},{192,160},{224,192},{256... | collective-permute-start | bytes 393224 | tf_op jit(solution)/shard_map/while/body/eval_jaxpr/ppermute | solution.py:13
  449.8 8.3 %collective-permute-start.1 = (f32[2,128,128]{2,1,0:T(8,128)}, f32[2,128,128]{2,1,0:T(8,128)S(1)}, u32[]{:S(2)}, u32[]{:S(2)}) collective-permute-start(f32[2,128,128]{2,1,0:T(8,128)} %multiply_add_fusion.11), channel_id=1, source_target_pairs={{32,0},{64,32},{96,64},{128,96},{160,128},{192,160},{224,192},{256... | collective-permute-start | bytes 393224 | tf_op jit(solution)/shard_map/while/body/eval_jaxpr/ppermute | solution.py:13
  (22 other events, 560.3 us)
where the time goes:
time: 473 us; the launch traced here: 471 us
  blocking collectives  158 us (33%)
  waiting for transfers between devices  138 us (29%)
  starting transfers between devices  112 us (24%)
  other arithmetic  29.4 us (6%)
  matrix products  20.7 us (4%)
  local copies, waits for them, and re-layouts  11.8 us (2%)
    ppermute x30, waiting for transfers between devices, passed_along(): lax.ppermute(value, axis, [(source, source + steps) for source in range(i...  138 us
    ppermute x30, starting transfers between devices, passed_along(): lax.ppermute(value, axis, [(source, source + steps) for source in range(i...  112 us
    psum x1, blocking collectives, local(): squares = lax.psum(jnp.sum(flattened * flattened, axis=1), 'head')  62.7 us
    psum x1, blocking collectives, local(): projected = lax.psum(jnp.sum(normed_grad * normed, axis=1), 'head')  62.7 us
    psum x1, blocking collectives, local(): gain_grad = lax.psum(gain_part, 'seq')  32.4 us
    add x15, other arithmetic, relay_step(): outgoing = jnp.exp(device_decay)[:, None, None] * suffix + device_back  21.1 us
  transfers between devices with their start and end apart: 30, of which 30 were waited for; matrix products, arithmetic and copies ran while one was open for 0% of the time, Pallas kernels for 0%

commit v1 on v0

v1 whole, which is shorter than its diff:
```python
import jax
import jax.numpy as jnp
from jax import lax
from jax.experimental import pallas as pl
from jax.experimental.pallas import tpu as pltpu
from jax.sharding import PartitionSpec as P

epsilon = 1e-06
width = 128
block_rows = 256
f32 = jnp.float32
bf16 = jnp.bfloat16


def dot(a, b, a_dim, b_dim):
    return lax.dot_general(a, b, (((a_dim,), (b_dim,)), ((), ())), preferred_element_type=f32)


def split(x):
    high = x.astype(bf16)
    return high, (x - high.astype(f32)).astype(bf16)


def side_by_side(x):
    return jnp.concatenate(split(x), axis=1)


def folded(x):
    return x[:, :width] + x[:, width:]


def dot_split_right(a, b, a_dim, b_dim):
    high, low = split(b)
    return dot(a, high, a_dim, b_dim) + dot(a, low, a_dim, b_dim)


def dot_split_left(a, b, a_dim, b_dim):
    high, low = split(a)
    return dot(high, b, a_dim, b_dim) + dot(low, b, a_dim, b_dim)


def dot_split_both(a, b, a_dim, b_dim):
    a_high, a_low = split(a)
    b_high, b_low = split(b)
    return (
        dot(a_high, b_high, a_dim, b_dim)
        + dot(a_high, b_low, a_dim, b_dim)
        + dot(a_low, b_high, a_dim, b_dim)
    )


def head_columns(ref, head):
    return ref[:, head * width : (head + 1) * width]


def block_of(array, block):
    return array[block * block_rows : (block + 1) * block_rows]


def start_column(table, block):
    return table[:, block : block + 1]


def end_column(table, block, blocks):
    return table[:, blocks + block : blocks + block + 1]


def inner_column(table, block, blocks):
    return table[:, 2 * blocks + block : 2 * blocks + block + 1]


def state_kernel(decay_ref, keys_ref, values_ref, pieces_ref, table_ref, rows_ref):
    heads, tokens = decay_ref.shape
    blocks = tokens // block_rows
    decay = decay_ref[...]
    stacked = jnp.concatenate(
        [
            decay[h : h + 1, b * block_rows : (b + 1) * block_rows]
            for h in range(heads)
            for b in range(blocks)
        ],
        axis=0,
    )
    row = lax.broadcasted_iota(jnp.int32, (block_rows, block_rows), 0)
    column = lax.broadcasted_iota(jnp.int32, (block_rows, block_rows), 1)
    upper = jnp.where(row <= column, 1.0, 0.0).astype(f32)
    sums = jnp.dot(stacked, upper, precision=lax.Precision.HIGHEST, preferred_element_type=f32)
    for h in range(heads):
        inside = sums[h * blocks : (h + 1) * blocks]
        offset = jnp.zeros((1, 1), f32)
        offsets = []
        for b in range(blocks):
            offsets.append(offset)
            offset = offset + inside[b : b + 1, block_rows - 1 : block_rows]
        from_device = inside + jnp.concatenate(offsets, axis=0)
        table = jnp.concatenate(
            [
                jnp.exp(from_device),
                jnp.exp(offset - from_device),
                inside,
                jnp.zeros((width - 3 * blocks, block_rows), f32),
            ],
            axis=0,
        ).T
        table_ref[h] = table
        rows_ref[h] = jnp.concatenate([inside, jnp.zeros((8 - blocks, block_rows), f32)], axis=0)
        values = head_columns(values_ref, h).astype(f32)
        weighted = jnp.concatenate(
            [
                side_by_side(end_column(table, b, blocks) * block_of(values, b))
                for b in range(blocks)
            ],
            axis=0,
        )
        state = folded(dot(head_columns(keys_ref, h), weighted, 0, 0))
        total = jnp.broadcast_to(jnp.exp(offset), (1, width))
        store_pieces(pieces_ref, h, heads, state, total)


def store_pieces(pieces_ref, head, heads, state, extra):
    count = heads * width // slice_rows(pieces_ref.shape[0], heads, extra.shape[0])
    rows = heads * width // count
    stride = rows + extra.shape[0]
    per_head = count // heads
    for index in range(per_head):
        base = (head * per_head + index) * stride
        pieces_ref[base : base + rows] = state[index * rows : (index + 1) * rows]
        pieces_ref[base + rows : base + stride] = extra


def slice_rows(total, heads, extra_rows):
    return heads * width * extra_rows // (total - heads * width)


def decay_mask(table, rows, block, blocks, causal):
    return jnp.exp(
        jnp.where(causal, inner_column(table, block, blocks) - rows[block : block + 1], -1e30)
    )


def causal_mask():
    row = lax.broadcasted_iota(jnp.int32, (block_rows, block_rows), 0)
    column = lax.broadcasted_iota(jnp.int32, (block_rows, block_rows), 1)
    return row >= column


def inside_kernel(queries_ref, keys_ref, values_ref, table_ref, rows_ref, local_ref):
    blocks = queries_ref.shape[0] // block_rows
    causal = causal_mask()
    table = table_ref[0]
    rows = rows_ref[0]
    running = None
    for b in range(blocks):
        part = slice(b * block_rows, (b + 1) * block_rows)
        query, key, value = queries_ref[part], keys_ref[part], values_ref[part]
        mask = decay_mask(table, rows, b, blocks, causal)
        inner = inner_column(table, b, blocks)
        total = inner[block_rows - 1 : block_rows]
        scores = dot(query, key, 1, 1) * mask
        result = dot_split_left(scores, value, 1, 0)
        if b:
            result = result + jnp.exp(inner) * folded(dot(query, side_by_side(running), 1, 0))
        local_ref[part] = result
        if b + 1 < blocks:
            weighted = jnp.exp(total - inner) * value.astype(f32)
            state = folded(dot(key, side_by_side(weighted), 0, 0))
            running = state if b == 0 else jnp.exp(total) * running + state


def prefix_kernel(pieces_ref, entering_ref, *, count):
    rows = entering_ref.shape[0] // count
    stride = pieces_ref.shape[0] // count
    prefix = jnp.zeros((rows, width), f32)
    for index in range(count):
        entering_ref[index * rows : (index + 1) * rows] = prefix
        base = index * stride
        if index + 1 < count:
            prefix = (
                pieces_ref[base + rows : base + rows + 1] * prefix
                + pieces_ref[base : base + rows]
            )


def suffix_kernel(decay_pieces_ref, pieces_ref, leaving_ref, gain_ref, *, count):
    rows = leaving_ref.shape[0] // count
    stride = pieces_ref.shape[0] // count
    decay_stride = decay_pieces_ref.shape[0] // count
    suffix = jnp.zeros((rows, width), f32)
    gain_sum = jnp.zeros(gain_ref.shape, f32)
    for index in reversed(range(count)):
        leaving_ref[index * rows : (index + 1) * rows] = suffix
        base = index * stride
        decay_row = index * decay_stride + rows
        suffix = (
            decay_pieces_ref[decay_row : decay_row + 1] * suffix + pieces_ref[base : base + rows]
        )
        gain_sum = gain_sum + pieces_ref[base + rows : base + stride]
    gain_ref[...] = gain_sum


def attend_kernel(
    queries_ref, grads_ref, gain_ref, local_ref, entering_ref, table_ref, attended_ref, sums_ref
):
    tokens, channels = queries_ref.shape
    heads = channels // width
    blocks = tokens // block_rows
    groups = tokens // width
    lane = lax.broadcasted_iota(jnp.int32, (width, width), 1)
    states = [side_by_side(entering_ref[h * width : (h + 1) * width]) for h in range(heads)]
    gathered = jnp.zeros((width, width), f32)
    for b in range(blocks):
        part = slice(b * block_rows, (b + 1) * block_rows)
        squares = jnp.zeros((block_rows, width), f32)
        products = jnp.zeros((block_rows, width), f32)
        for h in range(heads):
            cut = slice(h * width, (h + 1) * width)
            carried = folded(dot(queries_ref[part, cut], states[h], 1, 0))
            attended = local_ref[part, cut] + start_column(table_ref[h], b) * carried
            attended_ref[part, cut] = attended
            squares = squares + attended * attended
            products = products + grads_ref[part, cut].astype(f32) * gain_ref[:, cut] * attended
        square_sum = jnp.sum(squares, axis=1, keepdims=True)
        product_sum = jnp.sum(products, axis=1, keepdims=True)
        for piece in range(block_rows // width):
            group = b * (block_rows // width) + piece
            inner = slice(piece * width, (piece + 1) * width)
            gathered = jnp.where(lane == group, square_sum[inner], gathered)
            gathered = jnp.where(lane == groups + group, product_sum[inner], gathered)
    compact = gathered.T[: 2 * groups]
    for index in range(sums_ref.shape[0]):
        sums_ref[index] = compact


def grad_kernel(
    sums_ref, attended_ref, grads_ref, gain_ref, queries_ref, table_ref,
    output_ref, attended_grad_ref, pieces_ref, *, total_channels
):
    tokens, channels = queries_ref.shape
    heads = channels // width
    blocks = tokens // block_rows
    groups = tokens // width
    sums = sums_ref[0]
    for index in range(1, sums_ref.shape[0]):
        sums = sums + sums_ref[index]
    inverse = 1.0 / jnp.sqrt(sums[:groups] / total_channels + epsilon)
    mean = inverse * sums[groups:] / total_channels
    scales = jnp.concatenate(
        [inverse, mean, jnp.zeros((width - 2 * groups, width), f32)], axis=0
    ).T
    gain_rows = []
    backs = []
    for h in range(heads):
        cut = slice(h * width, (h + 1) * width)
        gain = gain_ref[:, cut]
        gain_sum = jnp.zeros((1, width), f32)
        weighted = []
        for group in range(groups):
            part = slice(group * width, (group + 1) * width)
            b = group * width // block_rows
            within = (group * width) % block_rows
            inverse_column = scales[:, group : group + 1]
            mean_column = scales[:, groups + group : groups + group + 1]
            grad = grads_ref[part, cut].astype(f32)
            normed = attended_ref[part, cut] * inverse_column
            output_ref[part, cut] = (normed * gain).astype(bf16)
            gain_sum = gain_sum + jnp.sum(grad * normed, axis=0, keepdims=True)
            attended_grad = (grad * gain - normed * mean_column) * inverse_column
            attended_grad_ref[part, cut] = attended_grad
            start = start_column(table_ref[h, within : within + width], b)
            weighted.append(side_by_side(start * attended_grad))
        gain_rows.append(gain_sum)
        backs.append(folded(dot(queries_ref[:, cut], jnp.concatenate(weighted, axis=0), 0, 0)))
    extra = jnp.concatenate(gain_rows, axis=0)
    for h in range(heads):
        store_pieces(pieces_ref, h, heads, backs[h], extra)


def local_grad_kernel(
    queries_ref, keys_ref, values_ref, attended_grad_ref, entering_ref, table_ref, rows_ref,
    query_grad_ref, key_part_ref, value_part_ref
):
    blocks = queries_ref.shape[0] // block_rows
    causal = causal_mask()
    table = table_ref[0]
    rows = rows_ref[0]
    entering = entering_ref[...]
    leaving = None
    for b in range(blocks):
        part = slice(b * block_rows, (b + 1) * block_rows)
        key, value = keys_ref[part], values_ref[part]
        grad_high, grad_low = split(attended_grad_ref[part])
        inner = inner_column(table, b, blocks)
        total = inner[block_rows - 1 : block_rows]
        mask = decay_mask(table, rows, b, blocks, causal)
        score_grad = (dot(grad_high, value, 1, 1) + dot(grad_low, value, 1, 1)) * mask
        state_high, state_low = split(entering)
        carried = (
            dot(grad_high, state_high, 1, 1)
            + dot(grad_high, state_low, 1, 1)
            + dot(grad_low, state_high, 1, 1)
        )
        score_high, score_low = split(score_grad)
        query_grad = dot(score_high, key, 1, 0) + dot(score_low, key, 1, 0)
        query_grad_ref[part] = (query_grad + jnp.exp(inner) * carried).astype(bf16)
        query = queries_ref[part]
        key_part_ref[part] = dot(score_high, query, 0, 0) + dot(score_low, query, 0, 0)
        scores = dot(query, key, 1, 1) * mask
        weights_high, weights_low = split(scores)
        value_part_ref[part] = (
            dot(weights_high, grad_high, 0, 0)
            + dot(weights_high, grad_low, 0, 0)
            + dot(weights_low, grad_high, 0, 0)
        )
        if b + 1 < blocks:
            weighted = jnp.exp(total - inner) * value.astype(f32)
            entering = jnp.exp(total) * entering + folded(dot(key, side_by_side(weighted), 0, 0))
    for b in reversed(range(blocks)):
        part = slice(b * block_rows, (b + 1) * block_rows)
        inner = inner_column(table, b, blocks)
        total = inner[block_rows - 1 : block_rows]
        to_end = jnp.exp(total - inner)
        if b + 1 < blocks:
            leave_high, leave_low = split(leaving)
            value = values_ref[part]
            key = keys_ref[part]
            key_part_ref[part] += to_end * (
                dot(value, leave_high, 1, 1) + dot(value, leave_low, 1, 1)
            )
            value_part_ref[part] += to_end * (
                dot(key, leave_high, 1, 0) + dot(key, leave_low, 1, 0)
            )
        if b:
            weighted = side_by_side(jnp.exp(inner) * attended_grad_ref[part])
            back = folded(dot(queries_ref[part], weighted, 0, 0))
            leaving = back if leaving is None else back + jnp.exp(total) * leaving


def finish_kernel(
    keys_ref, values_ref, leaving_ref, table_ref, key_part_ref, value_part_ref,
    key_grad_ref, value_grad_ref
):
    tokens, channels = keys_ref.shape
    heads = channels // width
    blocks = tokens // block_rows
    for h in range(heads):
        cut = slice(h * width, (h + 1) * width)
        high, low = split(leaving_ref[cut])
        across = jnp.concatenate([high, low], axis=1)
        down = jnp.concatenate([high, low], axis=0)
        for b in range(blocks):
            part = slice(b * block_rows, (b + 1) * block_rows)
            to_end = end_column(table_ref[h], b, blocks)
            key_carry = folded(dot(values_ref[part, cut], down, 1, 1))
            value_carry = folded(dot(keys_ref[part, cut], across, 1, 0))
            key_grad_ref[part, cut] = (key_part_ref[part, cut] + to_end * key_carry).astype(bf16)
            value_grad_ref[part, cut] = (
                value_part_ref[part, cut] + to_end * value_carry
            ).astype(bf16)


def shape(dims, dtype=f32):
    return jax.ShapeDtypeStruct(dims, dtype)


def exchange(pieces, count):
    flat = pieces.reshape(count, 1, pieces.shape[0] // count * width)
    return lax.all_to_all(flat, "seq", 0, 0, tiled=True).reshape(pieces.shape)


def local(queries, keys, values, log_decay, gain, out_grad):
    tokens, channels = queries.shape
    heads = log_decay.shape[0]
    seq_count = lax.axis_size("seq")
    head_count = lax.axis_size("head")
    total_channels = channels * head_count
    state_rows = heads * width
    gain_row = gain.reshape(1, channels)
    groups = tokens // width
    whole = pl.BlockSpec((tokens, width), lambda h: (0, h))
    table_spec = pl.BlockSpec((1, block_rows, width), lambda h: (h, 0, 0))
    rows_spec = pl.BlockSpec((1, 8, block_rows), lambda h: (h, 0, 0))
    state_spec = pl.BlockSpec((width, width), lambda h: (h, 0))

    pieces, table, rows = pl.pallas_call(
        state_kernel,
        out_shape=(
            shape((state_rows + seq_count, width)),
            shape((heads, block_rows, width)),
            shape((heads, 8, block_rows)),
        ),
        name="own_state",
    )(log_decay, keys, values)
    with jax.named_scope("scan_out"):
        arrived = exchange(pieces, seq_count)
    inside = pl.pallas_call(
        inside_kernel,
        out_shape=shape((tokens, channels)),
        grid=(heads,),
        in_specs=[whole, whole, whole, table_spec, rows_spec],
        out_specs=whole,
        cost_estimate=pl.CostEstimate(
            flops=2 * 4 * tokens * block_rows * channels, transcendentals=tokens * block_rows * heads,
            bytes_accessed=5 * tokens * channels * 2,
        ),
        name="inside",
    )(queries, keys, values, table, rows)
    prefixes = pl.pallas_call(
        lambda *refs: prefix_kernel(*refs, count=seq_count),
        out_shape=shape((state_rows, width)),
        name="prefix",
    )(arrived)
    with jax.named_scope("scan_back"):
        entering = exchange(prefixes, seq_count)
    attended, sums = pl.pallas_call(
        attend_kernel,
        out_shape=(shape((tokens, channels)), shape((head_count, 2 * groups, width))),
        name="attend",
    )(queries, out_grad, gain_row, inside, entering, table)
    with jax.named_scope("head_sums"):
        sums = lax.all_to_all(sums, "head", 0, 0, tiled=True)
    output, attended_grad, back_pieces = pl.pallas_call(
        lambda *refs: grad_kernel(*refs, total_channels=float(total_channels)),
        out_shape=(
            shape((tokens, channels), bf16),
            shape((tokens, channels)),
            shape((state_rows + heads * seq_count, width)),
        ),
        name="norm_grad",
    )(sums, attended, out_grad, gain_row, queries, table)
    with jax.named_scope("back_out"):
        back_arrived = exchange(back_pieces, seq_count)
    query_grad, key_part, value_part = pl.pallas_call(
        local_grad_kernel,
        out_shape=(
            shape((tokens, channels), bf16),
            shape((tokens, channels)),
            shape((tokens, channels)),
        ),
        grid=(heads,),
        in_specs=[whole, whole, whole, whole, state_spec, table_spec, rows_spec],
        out_specs=(whole, whole, whole),
        cost_estimate=pl.CostEstimate(
            flops=2 * 14 * tokens * block_rows * channels, transcendentals=tokens * block_rows * heads,
            bytes_accessed=14 * tokens * channels * 2,
        ),
        name="local_grad",
    )(queries, keys, values, attended_grad, entering, table, rows)
    suffixes, gain_sum = pl.pallas_call(
        lambda *refs: suffix_kernel(*refs, count=seq_count),
        out_shape=(shape((state_rows, width)), shape((heads, width))),
        name="suffix",
    )(arrived, back_arrived)
    with jax.named_scope("back_back"):
        leaving = exchange(suffixes, seq_count)
    key_grad, value_grad = pl.pallas_call(
        finish_kernel,
        out_shape=(shape((tokens, channels), bf16), shape((tokens, channels), bf16)),
        name="finish",
    )(keys, values, leaving, table, key_part, value_part)
    return output, query_grad, key_grad, value_grad, gain_sum.reshape(channels)


def solution(mesh):
    in_specs = (
        P("seq", "head"),
        P("seq", "head"),
        P("seq", "head"),
        P("head", "seq"),
        P("head"),
        P("seq", "head"),
    )
    out_specs = (P("seq", "head"), P("seq", "head"), P("seq", "head"), P("seq", "head"), P("head"))
    return jax.shard_map(local, mesh=mesh, in_specs=in_specs, out_specs=out_specs, check_vma=False)
```

time: 473 us -> 123 us (0.26)
  the two profiles are of different devices: /device:TPU:96 before, /device:TPU:32 now
where the time goes in v1:
time: 123 us
  blocking collectives  65.8 us (53%)
  Pallas kernels  31.6 us (26%)
  waiting for transfers between devices  13.7 us (11%)
  starting transfers between devices  9.47 us (8%)
  local copies, waits for them, and re-layouts  1.29 us (1%)
    all_to_all x2, blocking collectives, exchange(): return lax.all_to_all(flat, 'seq', 0, 0, tiled=True).reshape(pieces.shape)  49.4 us
    all_to_all x1, blocking collectives, local(): sums = lax.all_to_all(sums, 'head', 0, 0, tiled=True)  16.3 us
    all_to_all x2, waiting for transfers between devices, exchange(): return lax.all_to_all(flat, 'seq', 0, 0, tiled=True).reshape(pieces.shape)  13.7 us
    pallas_call x1, Pallas kernels, local(): pl.pallas_call(local_grad_kernel, out_shape=(shape((tokens, channels), bf...  10.2 us
    all_to_all x2, starting transfers between devices, exchange(): return lax.all_to_all(flat, 'seq', 0, 0, tiled=True).reshape(pieces.shape)  9.47 us
    pallas_call x1, Pallas kernels, local(): pl.pallas_call(inside_kernel, out_shape=shape((tokens, channels)), grid=(...  4.37 us
    pallas_call x1, Pallas kernels, local(): pl.pallas_call(finish_kernel, out_shape=(shape((tokens, channels), bf16),...  3.66 us
    pallas_call x1, Pallas kernels, local(): pl.pallas_call(lambda *refs: grad_kernel(*refs, total_channels=float(tota...  3.65 us
  transfers between devices with their start and end apart: 2, of which 2 were waited for; matrix products, arithmetic and copies ran while one was open for 0% of the time, Pallas kernels for 12%

profile of v1, /device:TPU:32, one launch (start us, length us, event | category | flops | bytes accessed | tf_op | source)
XLA Modules:
  0.0 122.5 jit_solution(4676204927721206867)
XLA Ops:
  0.6 3.0 %own_state.1 = (f32[272,128]{1,0:T(8,128)}, f32[2,256,128]{2,1,0:T(8,128)}, f32[2,8,256]{2,1,0:T(8,128)}) custom-call(f32[2,1024]{1,0:T(2,128)} %decay_ref.1, bf16[1024,256]{1,0:T(8,128)(2,1)} %keys_ref.7, bf16[1024,256]{1,0:T(8,128)(2,1)} %values_ref.7), custom_call_target="tpu_custom_call" | custom-call | tf_op jit(solution)/shard_map/own_state/pallas_call | solution.py:384
  3.7 29.6 %all_to_all.25 = f32[16,1,2176]{2,1,0:T(1,128)} all-to-all(f32[16,1,2176]{2,1,0:T(1,128)} %bitcast.18), channel_id=1, replica_groups=mesh['seq'=16,'head'=32] {'seq'}, dimensions={0} | all-to-all | bytes 278528 | tf_op jit(solution)/shard_map/scan_out/all_to_all | solution.py:367
  33.2 1.6 %prefix.1 = f32[256,128]{1,0:T(8,128)} custom-call(f32[272,128]{1,0:T(8,128)} %bitcast.10), custom_call_target="tpu_custom_call" | custom-call | tf_op jit(solution)/shard_map/prefix/pallas_call | solution.py:407
  34.8 4.6 %all-to-all-start.1 = ((f32[16,1,2048]{2,1,0:T(1,128)}), f32[16,1,2048]{2,1,0:T(1,128)S(1)}, u32[]{:S(2)}, u32[]{:S(2)}) async-start(f32[16,1,2048]{2,1,0:T(1,128)} %bitcast.16), calls=%async_computation.1 | async-start | bytes 262144 | tf_op jit(solution)/shard_map/scan_back/all_to_all | solution.py:367
  39.4 4.4 %inside.1.local_ref = f32[1024,256]{1,0:T(8,128)} custom-call(bf16[1024,256]{1,0:T(8,128)(2,1)} %queries_ref.5, bf16[1024,256]{1,0:T(8,128)(2,1)} %keys_ref.7, bf16[1024,256]{1,0:T(8,128)(2,1)} %values_ref.7, f32[2,256,128]{2,1,0:T(8,128)} %get-tuple-element.20.table_ref.refs_5_, f32[2,8,256]{2,1,0:T(8,128)} %get-tuple-element.21.rows_ref), custom_call_target="tpu_custom_call" | custom-call | flops 536870912 | bytes 2621440 | tf_op jit(solution)/shard_map/inside/pallas_call | solution.py:395
  43.8 9.5 %all-to-all-done.1 = f32[16,1,2048]{2,1,0:T(1,128)S(1)} async-done(((f32[16,1,2048]{2,1,0:T(1,128)}), f32[16,1,2048]{2,1,0:T(1,128)S(1)}, u32[]{:S(2)}, u32[]{:S(2)}) %all-to-all-start.1) | async-done | bytes 131104 | tf_op jit(solution)/shard_map/scan_back/all_to_all | solution.py:367
  53.3 0.0 copy-start.1
  53.3 0.7 copy-done.1
  54.0 3.4 %attend.1 = (f32[1024,256]{1,0:T(8,128)}, f32[32,16,128]{2,1,0:T(8,128)}) custom-call(bf16[1024,256]{1,0:T(8,128)(2,1)} %queries_ref.5, bf16[1024,256]{1,0:T(8,128)(2,1)} %refs_2_.1, f32[1,256]{1,0:T(1,128)} %bitcast.20, f32[1024,256]{1,0:T(8,128)} %inside.1.local_ref, f32[256,128]{1,0:T(8,128)} %bitcast.14, f32[2,256,128]{2,1,0:T(8,128)} %get-tuple-element.20.table_ref.refs_5_), custom_call_target="tpu_custom_call" | custom-call | tf_op jit(solution)/shard_map/attend/pallas_call | solution.py:414
  57.4 16.3 %all_to_all.26.refs_0_ = f32[32,16,128]{2,1,0:T(8,128)} all-to-all(f32[32,16,128]{2,1,0:T(8,128)} %get-tuple-element.23), channel_id=1, replica_groups=mesh['seq'=16,'head'=32] {'head'}, dimensions={0} | all-to-all | bytes 524288 | tf_op jit(solution)/shard_map/head_sums/all_to_all | solution.py:420
  73.7 3.7 %norm_grad.1 = (bf16[1024,256]{1,0:T(8,128)(2,1)}, f32[1024,256]{1,0:T(8,128)}, f32[288,128]{1,0:T(8,128)}) custom-call(f32[32,16,128]{2,1,0:T(8,128)} %all_to_all.26.refs_0_, f32[1024,256]{1,0:T(8,128)} %get-tuple-element.24.refs_1_, bf16[1024,256]{1,0:T(8,128)(2,1)} %refs_2_.1, f32[1,256]{1,0:T(1,128)} %bitcast.21, bf16[1024,256]{1,0:T(8,128)(2,1)} %queries_ref.5, ...), custom_call_target="tpu_custom_call" | custom-call | tf_op jit(solution)/shard_map/norm_grad/pallas_call | solution.py:421
  77.4 19.9 %all_to_all.27 = f32[16,1,2304]{2,1,0:T(1,128)} all-to-all(f32[16,1,2304]{2,1,0:T(1,128)} %bitcast.17), channel_id=1, replica_groups=mesh['seq'=16,'head'=32] {'seq'}, dimensions={0} | all-to-all | bytes 294912 | tf_op jit(solution)/shard_map/back_out/all_to_all | solution.py:367
  97.2 1.7 %suffix.1 = (f32[256,128]{1,0:T(8,128)}, f32[2,128]{1,0:T(2,128)}) custom-call(f32[272,128]{1,0:T(8,128)} %bitcast.11, f32[288,128]{1,0:T(8,128)} %bitcast.12), custom_call_target="tpu_custom_call" | custom-call | tf_op jit(solution)/shard_map/suffix/pallas_call | solution.py:448
  98.9 4.9 %all-to-all-start.4 = ((f32[16,1,2048]{2,1,0:T(1,128)}), f32[16,1,2048]{2,1,0:T(1,128)S(1)}, u32[]{:S(2)}, u32[]{:S(2)}) async-start(f32[16,1,2048]{2,1,0:T(1,128)} %bitcast.19), calls=%async_computation.4 | async-start | bytes 262144 | tf_op jit(solution)/shard_map/back_back/all_to_all | solution.py:367
  103.8 10.2 %local_grad.1 = (bf16[1024,256]{1,0:T(8,128)(2,1)}, f32[1024,256]{1,0:T(8,128)}, f32[1024,256]{1,0:T(8,128)}) custom-call(bf16[1024,256]{1,0:T(8,128)(2,1)} %queries_ref.5, bf16[1024,256]{1,0:T(8,128)(2,1)} %keys_ref.7, bf16[1024,256]{1,0:T(8,128)(2,1)} %values_ref.7, f32[1024,256]{1,0:T(8,128)} %get-tuple-element.26.attended_grad_ref, f32[256,128]{1,0:T(8,128)} %bitcast.15, ...), custom_call_target="tpu_custom_call" | custom-call | flops 1879048192 | bytes 7340032 | tf_op jit(solution)/shard_map/local_grad/pallas_call | solution.py:432
  114.0 4.2 %all-to-all-done.4 = f32[16,1,2048]{2,1,0:T(1,128)S(1)} async-done(((f32[16,1,2048]{2,1,0:T(1,128)}), f32[16,1,2048]{2,1,0:T(1,128)S(1)}, u32[]{:S(2)}, u32[]{:S(2)}) %all-to-all-start.4) | async-done | bytes 131104 | tf_op jit(solution)/shard_map/back_back/all_to_all | solution.py:367
  118.2 0.0 copy-start
  118.2 0.6 copy-done
  118.8 3.7 %finish.1 = (bf16[1024,256]{1,0:T(8,128)(2,1)}, bf16[1024,256]{1,0:T(8,128)(2,1)}) custom-call(bf16[1024,256]{1,0:T(8,128)(2,1)} %keys_ref.7, bf16[1024,256]{1,0:T(8,128)(2,1)} %values_ref.7, f32[256,128]{1,0:T(8,128)} %bitcast.13, f32[2,256,128]{2,1,0:T(8,128)} %get-tuple-element.20.table_ref.refs_5_, f32[1024,256]{1,0:T(8,128)} %get-tuple-element.30.key_part_ref, ...), custom_call_target="tpu_custom_call" | custom-call | tf_op jit(solution)/shard_map/finish/pallas_call | solution.py:455
Async XLA Ops:
  34.8 18.5 %all-to-all-start.1 = ((f32[16,1,2048]{2,1,0:T(1,128)}), f32[16,1,2048]{2,1,0:T(1,128)S(1)}, u32[]{:S(2)}, u32[]{:S(2)}) async-start(f32[16,1,2048]{2,1,0:T(1,128)} %bitcast.16), calls=%async_computation.1 | async-start | bytes 262144 | tf_op jit(solution)/shard_map/scan_back/all_to_all | solution.py:367
  53.3 0.7 copy-start.1
  98.9 19.3 %all-to-all-start.4 = ((f32[16,1,2048]{2,1,0:T(1,128)}), f32[16,1,2048]{2,1,0:T(1,128)S(1)}, u32[]{:S(2)}, u32[]{:S(2)}) async-start(f32[16,1,2048]{2,1,0:T(1,128)} %bitcast.19), calls=%async_computation.4 | async-start | bytes 262144 | tf_op jit(solution)/shard_map/back_back/all_to_all | solution.py:367
  118.2 0.6 copy-start

commit v2 on v1

v2 whole, which is shorter than its diff:
```python
import jax
import jax.numpy as jnp
from jax import lax
from jax.experimental import pallas as pl
from jax.experimental.pallas import tpu as pltpu
from jax.sharding import PartitionSpec as P

epsilon = 1e-06
width = 128
block_rows = 256
f32 = jnp.float32
bf16 = jnp.bfloat16


def dot(a, b, a_dim, b_dim):
    return lax.dot_general(a, b, (((a_dim,), (b_dim,)), ((), ())), preferred_element_type=f32)


def split(x):
    high = x.astype(bf16)
    return high, (x - high.astype(f32)).astype(bf16)


def side_by_side(x):
    return jnp.concatenate(split(x), axis=1)


def folded(x):
    return x[:, :width] + x[:, width:]


def dot_split_right(a, b, a_dim, b_dim):
    high, low = split(b)
    return dot(a, high, a_dim, b_dim) + dot(a, low, a_dim, b_dim)


def dot_split_left(a, b, a_dim, b_dim):
    high, low = split(a)
    return dot(high, b, a_dim, b_dim) + dot(low, b, a_dim, b_dim)


def dot_split_both(a, b, a_dim, b_dim):
    a_high, a_low = split(a)
    b_high, b_low = split(b)
    return (
        dot(a_high, b_high, a_dim, b_dim)
        + dot(a_high, b_low, a_dim, b_dim)
        + dot(a_low, b_high, a_dim, b_dim)
    )


def head_columns(ref, head):
    return ref[:, head * width : (head + 1) * width]


def block_of(array, block):
    return array[block * block_rows : (block + 1) * block_rows]


def table_column(table, kind, head, block, blocks):
    index = (3 * head + kind) * blocks + block
    return table[:, index : index + 1]


def start_column(table, head, block, blocks):
    return table_column(table, 0, head, block, blocks)


def end_column(table, head, block, blocks):
    return table_column(table, 1, head, block, blocks)


def inner_column(table, head, block, blocks):
    return table_column(table, 2, head, block, blocks)


def state_kernel(
    decay_ref, far_keys_ref, far_values_ref, pieces_ref, table_ref, rows_ref,
    keys_ref, values_ref, arrivals
):
    heads, tokens = decay_ref.shape
    values_in = pltpu.make_async_copy(far_values_ref, values_ref, arrivals.at[0])
    keys_in = pltpu.make_async_copy(far_keys_ref, keys_ref, arrivals.at[1])
    values_in.start()
    keys_in.start()
    blocks = tokens // block_rows
    decay = decay_ref[...]
    stacked = jnp.concatenate(
        [
            decay[h : h + 1, b * block_rows : (b + 1) * block_rows]
            for h in range(heads)
            for b in range(blocks)
        ],
        axis=0,
    )
    row = lax.broadcasted_iota(jnp.int32, (block_rows, block_rows), 0)
    column = lax.broadcasted_iota(jnp.int32, (block_rows, block_rows), 1)
    upper = jnp.where(row <= column, 1.0, 0.0).astype(f32)
    sums = jnp.dot(stacked, upper, precision=lax.Precision.HIGHEST, preferred_element_type=f32)
    table_rows = []
    totals = []
    for h in range(heads):
        inside = sums[h * blocks : (h + 1) * blocks]
        offset = jnp.zeros((1, 1), f32)
        offsets = []
        for b in range(blocks):
            offsets.append(offset)
            offset = offset + inside[b : b + 1, block_rows - 1 : block_rows]
        from_device = inside + jnp.concatenate(offsets, axis=0)
        table_rows += [jnp.exp(from_device), jnp.exp(offset - from_device), inside]
        totals.append(jnp.broadcast_to(jnp.exp(offset), (1, width)))
    table_rows.append(jnp.zeros((width - 3 * blocks * heads, block_rows), f32))
    table = jnp.concatenate(table_rows, axis=0).T
    table_ref[...] = table
    rows_ref[...] = sums
    values_in.wait()
    keys_in.wait()
    for h in range(heads):
        values = head_columns(values_ref, h).astype(f32)
        weighted = jnp.concatenate(
            [
                side_by_side(end_column(table, h, b, blocks) * block_of(values, b))
                for b in range(blocks)
            ],
            axis=0,
        )
        state = folded(dot(head_columns(keys_ref, h), weighted, 0, 0))
        store_pieces(pieces_ref, h, heads, state, totals[h])


def store_pieces(pieces_ref, head, heads, state, extra):
    count = heads * width // slice_rows(pieces_ref.shape[0], heads, extra.shape[0])
    rows = heads * width // count
    stride = rows + extra.shape[0]
    per_head = count // heads
    for index in range(per_head):
        base = (head * per_head + index) * stride
        pieces_ref[base : base + rows] = state[index * rows : (index + 1) * rows]
        pieces_ref[base + rows : base + stride] = extra


def slice_rows(total, heads, extra_rows):
    return heads * width * extra_rows // (total - heads * width)


def decay_mask(table, rows, head, block, blocks, causal):
    index = head * blocks + block
    inner = inner_column(table, head, block, blocks)
    return jnp.exp(jnp.where(causal, inner - rows[index : index + 1], -1e30))


def causal_mask():
    row = lax.broadcasted_iota(jnp.int32, (block_rows, block_rows), 0)
    column = lax.broadcasted_iota(jnp.int32, (block_rows, block_rows), 1)
    return row >= column


def inside_kernel(
    queries_ref, keys_ref, values_ref, table_ref, rows_ref, gain_in_ref,
    local_ref, gain_ref, order_ref
):
    tokens, channels = queries_ref.shape
    blocks = tokens // block_rows
    causal = causal_mask()
    table = table_ref[...]
    rows = rows_ref[...]
    for h in range(channels // width):
        cut = slice(h * width, (h + 1) * width)
        running = None
        for b in range(blocks):
            part = slice(b * block_rows, (b + 1) * block_rows)
            query, key, value = queries_ref[part, cut], keys_ref[part, cut], values_ref[part, cut]
            mask = decay_mask(table, rows, h, b, blocks, causal)
            inner = inner_column(table, h, b, blocks)
            total = inner[block_rows - 1 : block_rows]
            scores = dot(query, key, 1, 1) * mask
            result = dot_split_left(scores, value, 1, 0)
            if b:
                result = result + jnp.exp(inner) * folded(dot(query, side_by_side(running), 1, 0))
            local_ref[part, cut] = result
            if b + 1 < blocks:
                weighted = jnp.exp(total - inner) * value.astype(f32)
                state = folded(dot(key, side_by_side(weighted), 0, 0))
                running = state if b == 0 else jnp.exp(total) * running + state
    order_ref[...] = jnp.zeros(order_ref.shape, f32)
    gain_ref[...] = gain_in_ref[...]


def prefix_kernel(pieces_ref, order_ref, entering_ref, *, count):
    rows = entering_ref.shape[0] // count
    stride = pieces_ref.shape[0] // count
    prefix = jnp.zeros((rows, width), f32)
    for index in range(count):
        entering_ref[index * rows : (index + 1) * rows] = prefix
        base = index * stride
        if index + 1 < count:
            prefix = (
                pieces_ref[base + rows : base + rows + 1] * prefix
                + pieces_ref[base : base + rows]
            )


def suffix_kernel(
    decay_pieces_ref, pieces_ref, order_ref, leaving_ref, gain_ref, *, count
):
    rows = leaving_ref.shape[0] // count
    stride = pieces_ref.shape[0] // count
    decay_stride = decay_pieces_ref.shape[0] // count
    suffix = jnp.zeros((rows, width), f32)
    gain_sum = jnp.zeros(gain_ref.shape, f32)
    for index in reversed(range(count)):
        leaving_ref[index * rows : (index + 1) * rows] = suffix
        base = index * stride
        decay_row = index * decay_stride + rows
        suffix = (
            decay_pieces_ref[decay_row : decay_row + 1] * suffix + pieces_ref[base : base + rows]
        )
        gain_sum = gain_sum + pieces_ref[base + rows : base + stride]
    gain_ref[...] = gain_sum


def attend_kernel(
    queries_ref, grads_ref, gain_ref, local_ref, entering_ref, table_ref, attended_ref, sums_ref
):
    tokens, channels = queries_ref.shape
    heads = channels // width
    blocks = tokens // block_rows
    groups = tokens // width
    lane = lax.broadcasted_iota(jnp.int32, (width, width), 1)
    states = [side_by_side(entering_ref[h * width : (h + 1) * width]) for h in range(heads)]
    gathered = jnp.zeros((width, width), f32)
    for b in range(blocks):
        part = slice(b * block_rows, (b + 1) * block_rows)
        squares = jnp.zeros((block_rows, width), f32)
        products = jnp.zeros((block_rows, width), f32)
        for h in range(heads):
            cut = slice(h * width, (h + 1) * width)
            carried = folded(dot(queries_ref[part, cut], states[h], 1, 0))
            attended = local_ref[part, cut] + start_column(table_ref, h, b, blocks) * carried
            attended_ref[part, cut] = attended
            squares = squares + attended * attended
            products = products + grads_ref[part, cut].astype(f32) * gain_ref[:, cut] * attended
        square_sum = jnp.sum(squares, axis=1, keepdims=True)
        product_sum = jnp.sum(products, axis=1, keepdims=True)
        for piece in range(block_rows // width):
            group = b * (block_rows // width) + piece
            inner = slice(piece * width, (piece + 1) * width)
            gathered = jnp.where(lane == group, square_sum[inner], gathered)
            gathered = jnp.where(lane == groups + group, product_sum[inner], gathered)
    compact = gathered.T[: 2 * groups]
    for index in range(sums_ref.shape[0]):
        sums_ref[index] = compact


def grad_kernel(
    sums_ref, attended_ref, grads_ref, gain_ref, queries_ref, table_ref,
    far_grad_ref, far_scales_ref, pieces_ref, attended_grad_ref, scales_ref, departures,
    *, total_channels
):
    tokens, channels = queries_ref.shape
    heads = channels // width
    blocks = tokens // block_rows
    groups = tokens // width
    sums = sums_ref[0]
    for index in range(1, sums_ref.shape[0]):
        sums = sums + sums_ref[index]
    inverse = 1.0 / jnp.sqrt(sums[:groups] / total_channels + epsilon)
    mean = inverse * sums[groups:] / total_channels
    scales = jnp.concatenate(
        [inverse, mean, jnp.zeros((width - 2 * groups, width), f32)], axis=0
    ).T
    scales_ref[...] = scales
    leaving = [pltpu.make_async_copy(scales_ref, far_scales_ref, departures.at[heads])]
    leaving[0].start()
    gain_rows = []
    backs = []
    for h in range(heads):
        cut = slice(h * width, (h + 1) * width)
        gain = gain_ref[:, cut]
        gain_sum = jnp.zeros((1, width), f32)
        weighted = []
        for group in range(groups):
            part = slice(group * width, (group + 1) * width)
            b = group * width // block_rows
            within = (group * width) % block_rows
            inverse_column = scales[:, group : group + 1]
            mean_column = scales[:, groups + group : groups + group + 1]
            grad = grads_ref[part, cut].astype(f32)
            normed = attended_ref[part, cut] * inverse_column
            gain_sum = gain_sum + jnp.sum(grad * normed, axis=0, keepdims=True)
            attended_grad = (grad * gain - normed * mean_column) * inverse_column
            attended_grad_ref[part, cut] = attended_grad
            start = start_column(table_ref[within : within + width], h, b, blocks)
            weighted.append(side_by_side(start * attended_grad))
        out = pltpu.make_async_copy(
            attended_grad_ref.at[:, cut], far_grad_ref.at[:, cut], departures.at[h]
        )
        out.start()
        leaving.append(out)
        gain_rows.append(gain_sum)
        backs.append(folded(dot(queries_ref[:, cut], jnp.concatenate(weighted, axis=0), 0, 0)))
    extra = jnp.concatenate(gain_rows, axis=0)
    for h in range(heads):
        store_pieces(pieces_ref, h, heads, backs[h], extra)
    for out in leaving:
        out.wait()


def local_grad_kernel(
    attended_ref, gain_ref, scales_ref, queries_ref, keys_ref, values_ref, attended_grad_ref,
    entering_ref, table_ref, rows_ref,
    output_ref, query_grad_ref, key_part_ref, value_part_ref, order_ref
):
    tokens, channels = keys_ref.shape
    blocks = tokens // block_rows
    causal = causal_mask()
    table = table_ref[...]
    rows = rows_ref[...]
    for h in range(channels // width):
        cut = slice(h * width, (h + 1) * width)
        gain = gain_ref[:, cut]
        for group in range(tokens // width):
            part = slice(group * width, (group + 1) * width)
            normed = attended_ref[part, cut] * scales_ref[:, group : group + 1]
            output_ref[part, cut] = (normed * gain).astype(bf16)
        leaving = [None] * blocks
        for b in reversed(range(1, blocks)):
            part = slice(b * block_rows, (b + 1) * block_rows)
            inner = inner_column(table, h, b, blocks)
            total = inner[block_rows - 1 : block_rows]
            weighted = side_by_side(jnp.exp(inner) * attended_grad_ref[part, cut])
            back = folded(dot(queries_ref[part, cut], weighted, 0, 0))
            if leaving[b] is not None:
                back = back + jnp.exp(total) * leaving[b]
            leaving[b - 1] = back
        entering = entering_ref[cut]
        for b in range(blocks):
            part = slice(b * block_rows, (b + 1) * block_rows)
            query, key, value = queries_ref[part, cut], keys_ref[part, cut], values_ref[part, cut]
            grad_high, grad_low = split(attended_grad_ref[part, cut])
            inner = inner_column(table, h, b, blocks)
            total = inner[block_rows - 1 : block_rows]
            to_end = jnp.exp(total - inner)
            mask = decay_mask(table, rows, h, b, blocks, causal)
            score_grad = (dot(grad_high, value, 1, 1) + dot(grad_low, value, 1, 1)) * mask
            state_high, state_low = split(entering)
            carried = (
                dot(grad_high, state_high, 1, 1)
                + dot(grad_high, state_low, 1, 1)
                + dot(grad_low, state_high, 1, 1)
            )
            score_high, score_low = split(score_grad)
            query_grad = dot(score_high, key, 1, 0) + dot(score_low, key, 1, 0)
            query_grad_ref[part, cut] = (query_grad + jnp.exp(inner) * carried).astype(bf16)
            key_part = dot(score_high, query, 0, 0) + dot(score_low, query, 0, 0)
            weights_high, weights_low = split(dot(query, key, 1, 1) * mask)
            value_part = (
                dot(weights_high, grad_high, 0, 0)
                + dot(weights_high, grad_low, 0, 0)
                + dot(weights_low, grad_high, 0, 0)
            )
            if b + 1 < blocks:
                leave_high, leave_low = split(leaving[b])
                key_part = key_part + to_end * (
                    dot(value, leave_high, 1, 1) + dot(value, leave_low, 1, 1)
                )
                value_part = value_part + to_end * (
                    dot(key, leave_high, 1, 0) + dot(key, leave_low, 1, 0)
                )
                state = folded(dot(key, side_by_side(to_end * value.astype(f32)), 0, 0))
                entering = jnp.exp(total) * entering + state
            key_part_ref[part, cut] = key_part
            value_part_ref[part, cut] = value_part
    order_ref[...] = jnp.zeros(order_ref.shape, f32)


def finish_kernel(
    keys_ref, values_ref, leaving_ref, table_ref, key_part_ref, far_value_part_ref,
    far_key_grad_ref, far_value_grad_ref,
    value_part_ref, key_grad_ref, value_grad_ref, arrivals, departures
):
    tokens, channels = keys_ref.shape
    heads = channels // width
    blocks = tokens // block_rows
    parts = [slice(b * block_rows, (b + 1) * block_rows) for b in range(blocks)]
    arriving = []
    for b, part in enumerate(parts):
        copy = pltpu.make_async_copy(
            far_value_part_ref.at[part], value_part_ref.at[part], arrivals.at[b]
        )
        copy.start()
        arriving.append(copy)
    leaving = []

    def send(near_ref, far_ref, part):
        copy = pltpu.make_async_copy(
            near_ref.at[part], far_ref.at[part], departures.at[len(leaving)]
        )
        copy.start()
        leaving.append(copy)

    states = [split(leaving_ref[h * width : (h + 1) * width]) for h in range(heads)]
    for b, part in enumerate(parts):
        for h in range(heads):
            cut = slice(h * width, (h + 1) * width)
            down = jnp.concatenate(states[h], axis=0)
            carry = folded(dot(values_ref[part, cut], down, 1, 1))
            to_end = end_column(table_ref, h, b, blocks)
            key_grad_ref[part, cut] = (key_part_ref[part, cut] + to_end * carry).astype(bf16)
        send(key_grad_ref, far_key_grad_ref, part)
    for b, part in enumerate(parts):
        arriving[b].wait()
        for h in range(heads):
            cut = slice(h * width, (h + 1) * width)
            across = jnp.concatenate(states[h], axis=1)
            carry = folded(dot(keys_ref[part, cut], across, 1, 0))
            to_end = end_column(table_ref, h, b, blocks)
            value_grad_ref[part, cut] = (
                value_part_ref[part, cut] + to_end * carry
            ).astype(bf16)
        send(value_grad_ref, far_value_grad_ref, part)
    for copy in leaving:
        copy.wait()


def shape(dims, dtype=f32):
    return jax.ShapeDtypeStruct(dims, dtype)


def near(dims, dtype=f32):
    return pltpu.VMEM(dims, dtype)


class Held:
    def __init__(self, array):
        self.array = pltpu.with_memory_space_constraint(array, pltpu.VMEM)


def exchange(pieces, count):
    flat = pieces.reshape(count, 1, pieces.shape[0] // count * width)
    return lax.all_to_all(flat, "seq", 0, 0, tiled=True).reshape(pieces.shape)


class Far:
    def __init__(self, array):
        if isinstance(array, jax.ShapeDtypeStruct):
            self.array = pltpu.HBM(array.shape, array.dtype)
        else:
            self.array = pltpu.with_memory_space_constraint(array, pltpu.HBM)


def spec_of(item):
    if isinstance(item, Far):
        return pl.BlockSpec(memory_space=pltpu.HBM)
    if isinstance(item, Held):
        return pl.BlockSpec(memory_space=pltpu.VMEM)
    return pl.BlockSpec()


def bare(item):
    return item.array if isinstance(item, (Held, Far)) else item


def call(kernel, name, out_shape, operands, flops=0, scratch=()):
    return pl.pallas_call(
        kernel,
        out_shape=tuple(bare(x) for x in out_shape),
        in_specs=[spec_of(x) for x in operands],
        out_specs=tuple(spec_of(x) for x in out_shape),
        scratch_shapes=scratch,
        compiler_params=pltpu.CompilerParams(vmem_limit_bytes=24 * 2**20),
        cost_estimate=pl.CostEstimate(flops=flops, transcendentals=0, bytes_accessed=2**20),
        name=name,
    )(*(bare(x) for x in operands))


def local(queries, keys, values, log_decay, gain, out_grad):
    tokens, channels = queries.shape
    heads = log_decay.shape[0]
    seq_count = lax.axis_size("seq")
    head_count = lax.axis_size("head")
    total_channels = float(channels * head_count)
    state_rows = heads * width
    groups = tokens // width
    tile = (8, width)
    unit = 2 * tokens * block_rows * channels
    token_shape = (tokens, channels)

    pieces, table, rows = call(
        state_kernel, "own_state",
        (
            shape((state_rows + seq_count, width)),
            near((block_rows, width)),
            shape((heads * tokens // block_rows, block_rows)),
        ),
        (log_decay, Far(keys), Far(values)),
        scratch=(
            pltpu.VMEM(token_shape, bf16),
            pltpu.VMEM(token_shape, bf16),
            pltpu.SemaphoreType.DMA((2,)),
        ),
    )
    table = Held(table)
    with jax.named_scope("scan_out"):
        arrived = exchange(pieces, seq_count)
    inside, gain_row, order = call(
        inside_kernel, "inside", (near(token_shape), near((1, channels)), shape(tile)),
        (queries, keys, values, table, rows, gain.reshape(1, channels)), 4 * unit,
    )
    gain_row = Held(gain_row)
    arrived = Held(arrived)
    (prefixes,) = call(
        lambda *refs: prefix_kernel(*refs, count=seq_count), "prefix",
        (near((state_rows, width)),), (arrived, order),
    )
    with jax.named_scope("scan_back"):
        entering = Held(exchange(prefixes, seq_count))
    near_queries, near_grads = Held(queries), Held(out_grad)
    attended, sums = call(
        attend_kernel, "attend",
        (near(token_shape), near((head_count, 2 * groups, width))),
        (near_queries, near_grads, gain_row, Held(inside), entering, table),
    )
    with jax.named_scope("head_sums"):
        sums = Held(lax.all_to_all(sums, "head", 0, 0, tiled=True))
    attended_grad, scales, back_pieces = call(
        lambda *refs: grad_kernel(*refs, total_channels=total_channels), "norm_grad",
        (
            Far(shape(token_shape)),
            Far(shape((width, width))),
            shape((state_rows + heads * seq_count, width)),
        ),
        (sums, Held(attended), near_grads, gain_row, near_queries, table),
        scratch=(
            pltpu.VMEM(token_shape, f32),
            pltpu.VMEM((width, width), f32),
            pltpu.SemaphoreType.DMA((heads + 1,)),
        ),
    )
    with jax.named_scope("back_out"):
        back_arrived = exchange(back_pieces, seq_count)
    output, query_grad, key_part, value_part, order = call(
        local_grad_kernel, "local_grad",
        (
            shape(token_shape, bf16),
            shape(token_shape, bf16),
            shape(token_shape),
            shape(token_shape),
            shape(tile),
        ),
        (
            attended, gain_row, scales, queries, keys, values, attended_grad, entering,
            table, rows,
        ),
        15 * unit,
    )
    suffixes, gain_sum = call(
        lambda *refs: suffix_kernel(*refs, count=seq_count), "suffix",
        (near((state_rows, width)), shape((heads, width))),
        (arrived, Held(back_arrived), order),
    )
    with jax.named_scope("back_back"):
        leaving = Held(exchange(suffixes, seq_count))
    key_grad, value_grad = call(
        finish_kernel, "finish",
        (Far(shape(token_shape, bf16)), Far(shape(token_shape, bf16))),
        (Held(keys), Held(values), leaving, table, Held(key_part), Far(value_part)),
        scratch=(
            pltpu.VMEM(token_shape, f32),
            pltpu.VMEM(token_shape, bf16),
            pltpu.VMEM(token_shape, bf16),
            pltpu.SemaphoreType.DMA((tokens // block_rows,)),
            pltpu.SemaphoreType.DMA((2 * tokens // block_rows,)),
        ),
    )
    return output, query_grad, key_grad, value_grad, gain_sum.reshape(channels)


def solution(mesh):
    in_specs = (
        P("seq", "head"),
        P("seq", "head"),
        P("seq", "head"),
        P("head", "seq"),
        P("head"),
        P("seq", "head"),
    )
    out_specs = (P("seq", "head"), P("seq", "head"), P("seq", "head"), P("seq", "head"), P("head"))
    return jax.shard_map(local, mesh=mesh, in_specs=in_specs, out_specs=out_specs, check_vma=False)
```

time: 123 us -> 117 us (0.951)
  Pallas kernels: 31.6 us -> 19.5 us
  starting transfers between devices: 9.47 us -> 19.8 us
  blocking collectives: 65.8 us -> 56.8 us
  local copies, waits for them, and re-layouts: 1.29 us -> 5.93 us
    pallas_call x8, Pallas kernels: 31.6 us -> 19.5 us  [call(): pl.pallas_call(kernel, out_shape=tuple((bare(x) for x in out_shape)), in_...]
    all_to_all x2, starting transfers between devices: 9.47 us -> 19.8 us  [exchange(): return lax.all_to_all(flat, 'seq', 0, 0, tiled=True).reshape(pieces.shape)]
    all_to_all x2, blocking collectives: 49.4 us -> 40.8 us  [exchange(): return lax.all_to_all(flat, 'seq', 0, 0, tiled=True).reshape(pieces.shape)]
    unnamed x4 -> x28, local copies, waits for them, and re-layouts: 1.29 us -> 5.93 us
  transfers between devices with their start and end apart: 2 -> 2, of which waited for: 2 -> 2; matrix products, arithmetic and copies ran while one was open for 0% -> 0% of each run, Pallas kernels for 12% -> 9%
where the time goes in v2:
time: 117 us; the launch traced here: 116 us
  blocking collectives  56.8 us (49%)
  starting transfers between devices  19.8 us (17%)
  Pallas kernels  19.5 us (17%)
  waiting for transfers between devices  13.6 us (12%)
  local copies, waits for them, and re-layouts  5.93 us (5%)
    all_to_all x2, blocking collectives, exchange(): return lax.all_to_all(flat, 'seq', 0, 0, tiled=True).reshape(pieces.shape)  40.8 us
    all_to_all x2, starting transfers between devices, exchange(): return lax.all_to_all(flat, 'seq', 0, 0, tiled=True).reshape(pieces.shape)  19.8 us
    pallas_call x8, Pallas kernels, call(): pl.pallas_call(kernel, out_shape=tuple((bare(x) for x in out_shape)), in_...  19.5 us
    all_to_all x1, blocking collectives, local(): sums = Held(lax.all_to_all(sums, 'head', 0, 0, tiled=True))  16 us
    all_to_all x2, waiting for transfers between devices, exchange(): return lax.all_to_all(flat, 'seq', 0, 0, tiled=True).reshape(pieces.shape)  13.6 us
    unnamed x28, local copies, waits for them, and re-layouts  5.93 us
  transfers between devices with their start and end apart: 2, of which 2 were waited for; matrix products, arithmetic and copies ran while one was open for 0% of the time, Pallas kernels for 9%

profile of v2, /device:TPU:32, one launch (start us, length us, event | category | flops | bytes accessed | tf_op | source)
XLA Modules:
  0.0 116.5 jit_solution(12772929683957674626)
XLA Ops:
  0.6 0.0 copy-start.1
  0.6 0.0 copy-start
  0.7 0.0 copy-start.8
  0.7 0.8 copy-done.8
  1.4 2.5 %own_state.1 = (f32[272,128]{1,0:T(8,128)}, f32[256,128]{1,0:T(8,128)S(1)}, f32[8,256]{1,0:T(8,128)S(1)}) custom-call(f32[2,1024]{1,0:T(2,128)S(1)} %copy-done.8, bf16[1024,256]{1,0:T(8,128)(2,1)} %keys_ref.5, bf16[1024,256]{1,0:T(8,128)(2,1)} %values_ref.5), custom_call_target="tpu_custom_call" | custom-call | bytes 1048576 | tf_op jit(solution)/shard_map/own_state/pallas_call | solution.py:465
  3.9 0.0 copy-start.11
  4.0 15.2 %all-to-all-start = ((f32[16,1,2176]{2,1,0:T(1,128)}), f32[16,1,2176]{2,1,0:T(1,128)S(1)}, u32[]{:S(2)}, u32[]{:S(2)}) async-start(f32[16,1,2176]{2,1,0:T(1,128)} %bitcast.1), calls=%async_computation | async-start | bytes 278528 | tf_op jit(solution)/shard_map/scan_out/all_to_all | solution.py:441
  19.2 0.0 copy-done.11
  19.2 0.0 copy-done.1
  19.2 0.0 copy-done
  19.2 0.6 copy-done.13
  19.9 1.0 copy-done.3
  20.9 2.2 %inside.1 = (f32[1024,256]{1,0:T(8,128)S(1)}, f32[1,256]{1,0:T(1,128)S(1)}, f32[8,128]{1,0:T(8,128)S(1)}) custom-call(bf16[1024,256]{1,0:T(8,128)(2,1)S(1)} %copy-done.3, bf16[1024,256]{1,0:T(8,128)(2,1)S(1)} %copy-done, bf16[1024,256]{1,0:T(8,128)(2,1)S(1)} %copy-done.1, f32[256,128]{1,0:T(8,128)S(1)} %get-tuple-element.25.table_ref.refs_5_, ...), custom_call_target="tpu_custom_call" | custom-call | flops 536870912 | bytes 1048576 | tf_op jit(solution)/shard_map/inside/pallas_call | solution.py:465
  23.1 0.0 copy-start.2
  23.1 10.4 %all-to-all-done = f32[16,1,2176]{2,1,0:T(1,128)S(1)} async-done(((f32[16,1,2176]{2,1,0:T(1,128)}), f32[16,1,2176]{2,1,0:T(1,128)S(1)}, u32[]{:S(2)}, u32[]{:S(2)}) %all-to-all-start) | async-done | bytes 139296 | tf_op jit(solution)/shard_map/scan_out/all_to_all | solution.py:441
  33.6 18.1 %all_to_all.25 = f32[16,1,2048]{2,1,0:T(1,128)S(1)} all-to-all(f32[16,1,2048]{2,1,0:T(1,128)S(1)} %bitcast.15), channel_id=1, replica_groups=mesh['seq'=16,'head'=32] {'seq'}, dimensions={0} | all-to-all | bytes 262144 | tf_op jit(solution)/shard_map/scan_back/all_to_all | solution.py:441
  51.7 0.0 copy-done.4
  51.8 0.0 copy-done.2
  51.8 1.0 attend.1
  52.7 16.0 %all_to_all.26.refs_0_ = f32[32,16,128]{2,1,0:T(8,128)S(1)} all-to-all(f32[32,16,128]{2,1,0:T(8,128)S(1)} %get-tuple-element.32), channel_id=1, replica_groups=mesh['seq'=16,'head'=32] {'head'}, dimensions={0} | all-to-all | bytes 524288 | tf_op jit(solution)/shard_map/head_sums/all_to_all | solution.py:525
  68.8 2.6 %norm_grad.1 = (f32[1024,256]{1,0:T(8,128)}, f32[128,128]{1,0:T(8,128)}, f32[288,128]{1,0:T(8,128)}) custom-call(f32[32,16,128]{2,1,0:T(8,128)S(1)} %all_to_all.26.refs_0_, f32[1024,256]{1,0:T(8,128)S(1)} %get-tuple-element.31.refs_1_.attended_ref, bf16[1024,256]{1,0:T(8,128)(2,1)S(1)} %copy-done.2, f32[1,256]{1,0:T(1,128)S(1)} %get-tuple-element.27.gain_ref.refs_3_, ...), custom_call_target="tpu_custom_call" | custom-call | bytes 1048576 | tf_op jit(solution)/shard_map/norm_grad/pallas_call | solution.py:465
  71.4 0.0 copy-start.10
  71.4 0.0 copy-start.12
  71.4 4.6 %all-to-all-start.3 = ((f32[16,1,2304]{2,1,0:T(1,128)}), f32[16,1,2304]{2,1,0:T(1,128)S(1)}, u32[]{:S(2)}, u32[]{:S(2)}) async-start(f32[16,1,2304]{2,1,0:T(1,128)} %bitcast.5), calls=%async_computation.3 | async-start | bytes 294912 | tf_op jit(solution)/shard_map/back_out/all_to_all | solution.py:441
  76.0 1.2 %copy-done.7 = f32[1024,256]{1,0:T(8,128)S(1)} copy-done((f32[1024,256]{1,0:T(8,128)S(1)}, f32[1024,256]{1,0:T(8,128)}, u32[]{:S(2)}) %copy-start.7) | copy-done | bytes 1048600
  77.2 1.2 %copy-done.9 = f32[1024,256]{1,0:T(8,128)S(1)} copy-done((f32[1024,256]{1,0:T(8,128)S(1)}, f32[1024,256]{1,0:T(8,128)}, u32[]{:S(2)}) %copy-start.9) | copy-done | bytes 1048600
  78.4 8.0 %local_grad.1 = (bf16[1024,256]{1,0:T(8,128)(2,1)}, bf16[1024,256]{1,0:T(8,128)(2,1)}, f32[1024,256]{1,0:T(8,128)S(1)}, f32[1024,256]{1,0:T(8,128)S(1)}, f32[8,128]{1,0:T(8,128)S(1)}) custom-call(f32[1024,256]{1,0:T(8,128)S(1)} %copy-done.7, f32[1,256]{1,0:T(1,128)S(1)} %get-tuple-element.27.gain_ref.refs_3_, f32[128,128]{1,0:T(8,128)S(1)} %copy-done.10, ...), custom_call_target="tpu_custom_call" | custom-call | flops 2013265920 | bytes 1048576 | tf_op jit(solution)/shard_map/local_grad/pallas_call | solution.py:465
  86.4 1.0 copy-done.5
  87.4 3.1 %all-to-all-done.3 = f32[16,1,2304]{2,1,0:T(1,128)S(1)} async-done(((f32[16,1,2304]{2,1,0:T(1,128)}), f32[16,1,2304]{2,1,0:T(1,128)S(1)}, u32[]{:S(2)}, u32[]{:S(2)}) %all-to-all-start.3) | async-done | bytes 147488 | tf_op jit(solution)/shard_map/back_out/all_to_all | solution.py:441
  90.5 0.6 suffix.1
  91.1 22.7 %all_to_all.27 = f32[16,1,2048]{2,1,0:T(1,128)S(1)} all-to-all(f32[16,1,2048]{2,1,0:T(1,128)S(1)} %bitcast.17), channel_id=1, replica_groups=mesh['seq'=16,'head'=32] {'seq'}, dimensions={0} | all-to-all | bytes 262144 | tf_op jit(solution)/shard_map/back_back/all_to_all | solution.py:441
  113.8 2.7 %finish.1 = (bf16[1024,256]{1,0:T(8,128)(2,1)}, bf16[1024,256]{1,0:T(8,128)(2,1)}) custom-call(bf16[1024,256]{1,0:T(8,128)(2,1)S(1)} %copy-done, bf16[1024,256]{1,0:T(8,128)(2,1)S(1)} %copy-done.1, f32[256,128]{1,0:T(8,128)S(1)} %bitcast.16, f32[256,128]{1,0:T(8,128)S(1)} %get-tuple-element.25.table_ref.refs_5_, ...), custom_call_target="tpu_custom_call" | custom-call | bytes 1048576 | tf_op jit(solution)/shard_map/finish/pallas_call | solution.py:465
  (11 shorter events, 0.1 us)
Async XLA Ops:
  0.6 18.6 %copy-start.1 = (bf16[1024,256]{1,0:T(8,128)(2,1)S(1)}, bf16[1024,256]{1,0:T(8,128)(2,1)}, u32[]{:S(2)}) copy-start(bf16[1024,256]{1,0:T(8,128)(2,1)} %values_ref.5) | copy-start | bytes 1572868
  0.6 18.6 %copy-start = (bf16[1024,256]{1,0:T(8,128)(2,1)S(1)}, bf16[1024,256]{1,0:T(8,128)(2,1)}, u32[]{:S(2)}) copy-start(bf16[1024,256]{1,0:T(8,128)(2,1)} %keys_ref.5) | copy-start | bytes 1572868
  0.7 0.8 copy-start.8
  3.9 15.2 %copy-start.11 = (f32[8,256]{1,0:T(8,128)}, f32[8,256]{1,0:T(8,128)S(1)}, u32[]{:S(2)}) copy-start(f32[8,256]{1,0:T(8,128)S(1)} %get-tuple-element.26.rows_ref) | copy-start | bytes 24580
  4.0 29.6 %all-to-all-start = ((f32[16,1,2176]{2,1,0:T(1,128)}), f32[16,1,2176]{2,1,0:T(1,128)S(1)}, u32[]{:S(2)}, u32[]{:S(2)}) async-start(f32[16,1,2176]{2,1,0:T(1,128)} %bitcast.1), calls=%async_computation | async-start | bytes 278528 | tf_op jit(solution)/shard_map/scan_out/all_to_all | solution.py:441
  19.2 0.7 copy-start.13
  19.9 1.0 copy-start.3
  20.9 30.8 %copy-start.4 = (bf16[1024,256]{1,0:T(8,128)(2,1)S(1)}, bf16[1024,256]{1,0:T(8,128)(2,1)}, u32[]{:S(2)}) copy-start(bf16[1024,256]{1,0:T(8,128)(2,1)} %queries_ref.5) | copy-start | bytes 1572868
  23.1 28.6 %copy-start.2 = (bf16[1024,256]{1,0:T(8,128)(2,1)S(1)}, bf16[1024,256]{1,0:T(8,128)(2,1)}, u32[]{:S(2)}) copy-start(bf16[1024,256]{1,0:T(8,128)(2,1)} %refs_2_.1) | copy-start | bytes 1572868
  52.7 18.6 %copy-start.6 = (f32[1024,256]{1,0:T(8,128)}, f32[1024,256]{1,0:T(8,128)S(1)}, u32[]{:S(2)}) copy-start(f32[1024,256]{1,0:T(8,128)S(1)} %get-tuple-element.31.refs_1_.attended_ref) | copy-start | bytes 3145732
  71.4 4.6 %copy-start.10 = (f32[128,128]{1,0:T(8,128)S(1)}, f32[128,128]{1,0:T(8,128)}, u32[]{:S(2)}) copy-start(f32[128,128]{1,0:T(8,128)} %get-tuple-element.33.scales_ref) | copy-start | bytes 196612
  71.4 4.6 %copy-start.12 = (f32[8,256]{1,0:T(8,128)S(1)}, f32[8,256]{1,0:T(8,128)}, u32[]{:S(2)}) copy-start(f32[8,256]{1,0:T(8,128)} %copy-done.11) | copy-start | bytes 24580
  71.4 19.1 %all-to-all-start.3 = ((f32[16,1,2304]{2,1,0:T(1,128)}), f32[16,1,2304]{2,1,0:T(1,128)S(1)}, u32[]{:S(2)}, u32[]{:S(2)}) async-start(f32[16,1,2304]{2,1,0:T(1,128)} %bitcast.5), calls=%async_computation.3 | async-start | bytes 294912 | tf_op jit(solution)/shard_map/back_out/all_to_all | solution.py:441
  76.0 1.2 %copy-start.7 = (f32[1024,256]{1,0:T(8,128)S(1)}, f32[1024,256]{1,0:T(8,128)}, u32[]{:S(2)}) copy-start(f32[1024,256]{1,0:T(8,128)} %copy-done.6) | copy-start | bytes 3145732
  77.2 1.2 %copy-start.9 = (f32[1024,256]{1,0:T(8,128)S(1)}, f32[1024,256]{1,0:T(8,128)}, u32[]{:S(2)}) copy-start(f32[1024,256]{1,0:T(8,128)} %get-tuple-element.34.attended_grad_ref) | copy-start | bytes 3145732
  86.4 1.0 copy-start.5

commit v3 on v2

--- a/solution.py
+++ b/solution.py
@@ -75,14 +75,17 @@
 
 
 def state_kernel(
-    decay_ref, far_keys_ref, far_values_ref, pieces_ref, table_ref, rows_ref,
-    keys_ref, values_ref, arrivals
+    far_decay_ref, far_keys_ref, far_values_ref, pieces_ref, table_ref, rows_ref,
+    decay_ref, keys_ref, values_ref, arrivals
 ):
     heads, tokens = decay_ref.shape
+    decay_in = pltpu.make_async_copy(far_decay_ref, decay_ref, arrivals.at[2])
+    decay_in.start()
     values_in = pltpu.make_async_copy(far_values_ref, values_ref, arrivals.at[0])
     keys_in = pltpu.make_async_copy(far_keys_ref, keys_ref, arrivals.at[1])
     values_in.start()
     keys_in.start()
+    decay_in.wait()
     blocks = tokens // block_rows
     decay = decay_ref[...]
     stacked = jnp.concatenate(
@@ -155,20 +158,59 @@
     return row >= column
 
 
+def row_blocks(tokens):
+    return [slice(b * block_rows, (b + 1) * block_rows) for b in range(tokens // block_rows)]
+
+
+def stream_in(far_refs, near_refs, arrivals, order, parts):
+    copies = {}
+    for b in order:
+        copies[b] = [
+            pltpu.make_async_copy(far.at[parts[b]], near.at[parts[b]], arrivals.at[index, b])
+            for index, (far, near) in enumerate(zip(far_refs, near_refs))
+        ]
+        for copy in copies[b]:
+            copy.start()
+    return copies
+
+
+def stream_out(near_refs, far_refs, departures, b, part):
+    copies = [
+        pltpu.make_async_copy(near.at[part], far.at[part], departures.at[index, b])
+        for index, (far, near) in enumerate(zip(far_refs, near_refs))
+    ]
+    for copy in copies:
+        copy.start()
+    return copies
+
+
+def wait_all(copies):
+    for copy in copies:
+        copy.wait()
+
+
 def inside_kernel(
-    queries_ref, keys_ref, values_ref, table_ref, rows_ref, gain_in_ref,
-    local_ref, gain_ref, order_ref
+    far_queries_ref, far_keys_ref, far_values_ref, table_ref, rows_ref, gain_in_ref,
+    local_ref, gain_ref, order_ref, queries_ref, keys_ref, values_ref, arrivals
 ):
     tokens, channels = queries_ref.shape
-    blocks = tokens // block_rows
+    heads = channels // width
+    parts = row_blocks(tokens)
+    blocks = len(parts)
+    arriving = stream_in(
+        (far_queries_ref, far_keys_ref, far_values_ref),
+        (queries_ref, keys_ref, values_ref), arrivals, range(blocks), parts,
+    )
     causal = causal_mask()
     table = table_ref[...]
     rows = rows_ref[...]
-    for h in range(channels // width):
-        cut = slice(h * width, (h + 1) * width)
-        running = None
-        for b in range(blocks):
-            part = slice(b * block_rows, (b + 1) * block_rows)
+    order_ref[...] = jnp.zeros(order_ref.shape, f32)
+    gain_ref[...] = gain_in_ref[...]
+    running = [None] * heads
+    for b, part in enumerate(parts):
+        wait_all(arriving[b])
+        for h in range(heads):
+            cut = slice(h * width, (h + 1) * width)
             query, key, value = queries_ref[part, cut], keys_ref[part, cut], values_ref[part, cut]
             mask = decay_mask(table, rows, h, b, blocks, causal)
             inner = inner_column(table, h, b, blocks)
@@ -176,14 +218,13 @@
             scores = dot(query, key, 1, 1) * mask
             result = dot_split_left(scores, value, 1, 0)
             if b:
-                result = result + jnp.exp(inner) * folded(dot(query, side_by_side(running), 1, 0))
+                carried = folded(dot(query, side_by_side(running[h]), 1, 0))
+                result = result + jnp.exp(inner) * carried
             local_ref[part, cut] = result
             if b + 1 < blocks:
                 weighted = jnp.exp(total - inner) * value.astype(f32)
                 state = folded(dot(key, side_by_side(weighted), 0, 0))
-                running = state if b == 0 else jnp.exp(total) * running + state
-    order_ref[...] = jnp.zeros(order_ref.shape, f32)
-    gain_ref[...] = gain_in_ref[...]
+                running[h] = state if b == 0 else jnp.exp(total) * running[h] + state
 
 
 def prefix_kernel(pieces_ref, order_ref, entering_ref, *, count):
@@ -306,53 +347,40 @@
         out.wait()
 
 
-def local_grad_kernel(
-    attended_ref, gain_ref, scales_ref, queries_ref, keys_ref, values_ref, attended_grad_ref,
-    entering_ref, table_ref, rows_ref,
-    output_ref, query_grad_ref, key_part_ref, value_part_ref, order_ref
+def key_value_kernel(
+    far_queries_ref, far_keys_ref, far_values_ref, far_grad_ref, table_ref, rows_ref,
+    far_key_part_ref, far_value_part_ref, order_ref,
+    queries_ref, keys_ref, values_ref, grad_ref, key_part_ref, value_part_ref,
+    arrivals, departures
 ):
     tokens, channels = keys_ref.shape
-    blocks = tokens // block_rows
+    heads = channels // width
+    parts = row_blocks(tokens)
+    blocks = len(parts)
+    backward = list(reversed(range(blocks)))
+    arriving = stream_in(
+        (far_queries_ref, far_keys_ref, far_values_ref, far_grad_ref),
+        (queries_ref, keys_ref, values_ref, grad_ref), arrivals, backward, parts,
+    )
     causal = causal_mask()
     table = table_ref[...]
     rows = rows_ref[...]
-    for h in range(channels // width):
-        cut = slice(h * width, (h + 1) * width)
-        gain = gain_ref[:, cut]
-        for group in range(tokens // width):
-            part = slice(group * width, (group + 1) * width)
-            normed = attended_ref[part, cut] * scales_ref[:, group : group + 1]
-            output_ref[part, cut] = (normed * gain).astype(bf16)
-        leaving = [None] * blocks
-        for b in reversed(range(1, blocks)):
-            part = slice(b * block_rows, (b + 1) * block_rows)
+    order_ref[...] = jnp.zeros(order_ref.shape, f32)
+    leaving = [None] * heads
+    departing = []
+    for b in backward:
+        part = parts[b]
+        wait_all(arriving[b])
+        for h in range(heads):
+            cut = slice(h * width, (h + 1) * width)
+            query, key, value = queries_ref[part, cut], keys_ref[part, cut], values_ref[part, cut]
+            grad = grad_ref[part, cut]
+            grad_high, grad_low = split(grad)
             inner = inner_column(table, h, b, blocks)
             total = inner[block_rows - 1 : block_rows]
-            weighted = side_by_side(jnp.exp(inner) * attended_grad_ref[part, cut])
-            back = folded(dot(queries_ref[part, cut], weighted, 0, 0))
-            if leaving[b] is not None:
-                back = back + jnp.exp(total) * leaving[b]
-            leaving[b - 1] = back
-        entering = entering_ref[cut]
-        for b in range(blocks):
-            part = slice(b * block_rows, (b + 1) * block_rows)
-            query, key, value = queries_ref[part, cut], keys_ref[part, cut], values_ref[part, cut]
-            grad_high, grad_low = split(attended_grad_ref[part, cut])
-            inner = inner_column(table, h, b, blocks)
-            total = inner[block_rows - 1 : block_rows]
-            to_end = jnp.exp(total - inner)
             mask = decay_mask(table, rows, h, b, blocks, causal)
             score_grad = (dot(grad_high, value, 1, 1) + dot(grad_low, value, 1, 1)) * mask
-            state_high, state_low = split(entering)
-            carried = (
-                dot(grad_high, state_high, 1, 1)
-                + dot(grad_high, state_low, 1, 1)
-                + dot(grad_low, state_high, 1, 1)
-            )
-            score_high, score_low = split(score_grad)
-            query_grad = dot(score_high, key, 1, 0) + dot(score_low, key, 1, 0)
-            query_grad_ref[part, cut] = (query_grad + jnp.exp(inner) * carried).astype(bf16)
-            key_part = dot(score_high, query, 0, 0) + dot(score_low, query, 0, 0)
+            key_part = dot_split_left(score_grad, query, 0, 0)
             weights_high, weights_low = split(dot(query, key, 1, 1) * mask)
             value_part = (
                 dot(weights_high, grad_high, 0, 0)
@@ -360,67 +388,111 @@
                 + dot(weights_low, grad_high, 0, 0)
             )
             if b + 1 < blocks:
-                leave_high, leave_low = split(leaving[b])
+                to_end = jnp.exp(total - inner)
+                leave_high, leave_low = split(leaving[h])
                 key_part = key_part + to_end * (
                     dot(value, leave_high, 1, 1) + dot(value, leave_low, 1, 1)
                 )
                 value_part = value_part + to_end * (
                     dot(key, leave_high, 1, 0) + dot(key, leave_low, 1, 0)
                 )
-                state = folded(dot(key, side_by_side(to_end * value.astype(f32)), 0, 0))
-                entering = jnp.exp(total) * entering + state
             key_part_ref[part, cut] = key_part
             value_part_ref[part, cut] = value_part
-    order_ref[...] = jnp.zeros(order_ref.shape, f32)
-
-
-def finish_kernel(
-    keys_ref, values_ref, leaving_ref, table_ref, key_part_ref, far_value_part_ref,
-    far_key_grad_ref, far_value_grad_ref,
-    value_part_ref, key_grad_ref, value_grad_ref, arrivals, departures
+            if b:
+                back = folded(dot(query, side_by_side(jnp.exp(inner) * grad), 0, 0))
+                leaving[h] = back if b + 1 == blocks else back + jnp.exp(total) * leaving[h]
+        departing += stream_out(
+            (key_part_ref, value_part_ref), (far_key_part_ref, far_value_part_ref),
+            departures, b, part,
+        )
+    wait_all(departing)
+
+
+def query_kernel(
+    far_attended_ref, far_grad_ref, far_keys_ref, far_values_ref, gain_ref, scales_ref,
+    entering_ref, table_ref, rows_ref, order_ref, far_output_ref, far_query_grad_ref,
+    attended_ref, grad_ref, keys_ref, values_ref, output_ref, query_grad_ref,
+    arrivals, departures
 ):
     tokens, channels = keys_ref.shape
     heads = channels // width
-    blocks = tokens // block_rows
-    parts = [slice(b * block_rows, (b + 1) * block_rows) for b in range(blocks)]
-    arriving = []
+    parts = row_blocks(tokens)
+    blocks = len(parts)
+    arriving = stream_in(
+        (far_attended_ref, far_grad_ref, far_keys_ref, far_values_ref),
+        (attended_ref, grad_ref, keys_ref, values_ref), arrivals, range(blocks), parts,
+    )
+    causal = causal_mask()
+    table = table_ref[...]
+    rows = rows_ref[...]
+    entering = [entering_ref[h * width : (h + 1) * width] for h in range(heads)]
+    departing = []
     for b, part in enumerate(parts):
-        copy = pltpu.make_async_copy(
-            far_value_part_ref.at[part], value_part_ref.at[part], arrivals.at[b]
-        )
-        copy.start()
-        arriving.append(copy)
-    leaving = []
-
-    def send(near_ref, far_ref, part):
-        copy = pltpu.make_async_copy(
-            near_ref.at[part], far_ref.at[part], departures.at[len(leaving)]
-        )
-        copy.start()
-        leaving.append(copy)
-
-    states = [split(leaving_ref[h * width : (h + 1) * width]) for h in range(heads)]
-    for b, part in enumerate(parts):
+        wait_all(arriving[b])
+        for group in range(b * block_rows // width, (b + 1) * block_rows // width):
+            piece = slice(group * width, (group + 1) * width)
+            normed = attended_ref[piece] * scales_ref[:, group : group + 1]
+            output_ref[piece] = (normed * gain_ref[...]).astype(bf16)
         for h in range(heads):
             cut = slice(h * width, (h + 1) * width)
-            down = jnp.concatenate(states[h], axis=0)
-            carry = folded(dot(values_ref[part, cut], down, 1, 1))
-            to_end = end_column(table_ref, h, b, blocks)
-            key_grad_ref[part, cut] = (key_part_ref[part, cut] + to_end * carry).astype(bf16)
-        send(key_grad_ref, far_key_grad_ref, part)
+            key, value = keys_ref[part, cut], values_ref[part, cut]
+            grad_high, grad_low = split(grad_ref[part, cut])
+            inner = inner_column(table, h, b, blocks)
+            total = inner[block_rows - 1 : block_rows]
+            mask = decay_mask(table, rows, h, b, blocks, causal)
+            score_grad = (dot(grad_high, value, 1, 1) + dot(grad_low, value, 1, 1)) * mask
+            state_high, state_low = split(entering[h])
+            carried = (
+                dot(grad_high, state_high, 1, 1)
+                + dot(grad_high, state_low, 1, 1)
+                + dot(grad_low, state_high, 1, 1)
+            )
+            query_grad = dot_split_left(score_grad, key, 1, 0) + jnp.exp(inner) * carried
+            query_grad_ref[part, cut] = query_grad.astype(bf16)
+            if b + 1 < blocks:
+                weighted = jnp.exp(total - inner) * value.astype(f32)
+                state = folded(dot(key, side_by_side(weighted), 0, 0))
+                entering[h] = jnp.exp(total) * entering[h] + state
+        departing += stream_out(
+            (output_ref, query_grad_ref), (far_output_ref, far_query_grad_ref),
+            departures, b, part,
+        )
+    wait_all(departing)
+
+
+def finish_kernel(
+    keys_ref, values_ref, leaving_ref, table_ref, far_key_part_ref, far_value_part_ref,
+    far_key_grad_ref, far_value_grad_ref,
+    key_part_ref, value_part_ref, key_grad_ref, value_grad_ref, arrivals, departures
+):
+    tokens, channels = keys_ref.shape
+    heads = channels // width
+    parts = row_blocks(tokens)
+    blocks = len(parts)
+    arriving = stream_in(
+        (far_key_part_ref, far_value_part_ref), (key_part_ref, value_part_ref),
+        arrivals, range(blocks), parts,
+    )
+    states = [split(leaving_ref[h * width : (h + 1) * width]) for h in range(heads)]
+    departing = []
     for b, part in enumerate(parts):
-        arriving[b].wait()
+        wait_all(arriving[b])
         for h in range(heads):
             cut = slice(h * width, (h + 1) * width)
             across = jnp.concatenate(states[h], axis=1)
-            carry = folded(dot(keys_ref[part, cut], across, 1, 0))
+            down = jnp.concatenate(states[h], axis=0)
             to_end = end_column(table_ref, h, b, blocks)
+            key_carry = folded(dot(values_ref[part, cut], down, 1, 1))
+            value_carry = folded(dot(keys_ref[part, cut], across, 1, 0))
+            key_grad_ref[part, cut] = (key_part_ref[part, cut] + to_end * key_carry).astype(bf16)
             value_grad_ref[part, cut] = (
-                value_part_ref[part, cut] + to_end * carry
+                value_part_ref[part, cut] + to_end * value_carry
             ).astype(bf16)
-        send(value_grad_ref, far_value_grad_ref, part)
-    for copy in leaving:
-        copy.wait()
+        departing += stream_out(
+            (key_grad_ref, value_grad_ref), (far_key_grad_ref, far_value_grad_ref),
+            departures, b, part,
+        )
+    wait_all(departing)
 
 
 def shape(dims, dtype=f32):
@@ -485,6 +557,9 @@
     tile = (8, width)
     unit = 2 * tokens * block_rows * channels
     token_shape = (tokens, channels)
+    blocks = tokens // block_rows
+    narrow = pltpu.VMEM(token_shape, bf16)
+    wide = pltpu.VMEM(token_shape, f32)
 
     pieces, table, rows = call(
         state_kernel, "own_state",
@@ -493,11 +568,12 @@
             near((block_rows, width)),
             shape((heads * tokens // block_rows, block_rows)),
         ),
-        (log_decay, Far(keys), Far(values)),
+        (Far(log_decay), Far(keys), Far(values)),
         scratch=(
+            pltpu.VMEM(log_decay.shape, f32),
             pltpu.VMEM(token_shape, bf16),
             pltpu.VMEM(token_shape, bf16),
-            pltpu.SemaphoreType.DMA((2,)),
+            pltpu.SemaphoreType.DMA((3,)),
         ),
     )
     table = Held(table)
@@ -505,7 +581,8 @@
         arrived = exchange(pieces, seq_count)
     inside, gain_row, order = call(
         inside_kernel, "inside", (near(token_shape), near((1, channels)), shape(tile)),
-        (queries, keys, values, table, rows, gain.reshape(1, channels)), 4 * unit,
+        (Far(queries), Far(keys), Far(values), table, rows, gain.reshape(1, channels)), 4 * unit,
+        scratch=(narrow, narrow, narrow, pltpu.SemaphoreType.DMA((3, blocks))),
     )
     gain_row = Held(gain_row)
     arrived = Held(arrived)
@@ -539,38 +616,45 @@
     )
     with jax.named_scope("back_out"):
         back_arrived = exchange(back_pieces, seq_count)
-    output, query_grad, key_part, value_part, order = call(
-        local_grad_kernel, "local_grad",
-        (
-            shape(token_shape, bf16),
-            shape(token_shape, bf16),
-            shape(token_shape),
-            shape(token_shape),
-            shape(tile),
-        ),
-        (
-            attended, gain_row, scales, queries, keys, values, attended_grad, entering,
-            table, rows,
-        ),
-        15 * unit,
+    key_part, value_part, order = call(
+        key_value_kernel, "key_value",
+        (Far(shape(token_shape)), Far(shape(token_shape)), shape(tile)),
+        (Far(queries), Far(keys), Far(values), Far(attended_grad), table, rows), 9 * unit,
+        scratch=(
+            narrow, narrow, narrow, wide, wide, wide,
+            pltpu.SemaphoreType.DMA((4, blocks)),
+            pltpu.SemaphoreType.DMA((2, blocks)),
+        ),
     )
     suffixes, gain_sum = call(
         lambda *refs: suffix_kernel(*refs, count=seq_count), "suffix",
-        (near((state_rows, width)), shape((heads, width))),
+        (shape((state_rows, width)), shape((heads, width))),
         (arrived, Held(back_arrived), order),
     )
     with jax.named_scope("back_back"):
         leaving = Held(exchange(suffixes, seq_count))
+    output, query_grad = call(
+        query_kernel, "query_grad",
+        (Far(shape(token_shape, bf16)), Far(shape(token_shape, bf16))),
+        (
+            Far(attended), Far(attended_grad), Far(keys), Far(values), gain_row, scales,
+            entering, table, rows, gain_sum,
+        ),
+        7 * unit,
+        scratch=(
+            wide, wide, narrow, narrow, narrow, narrow,
+            pltpu.SemaphoreType.DMA((4, blocks)),
+            pltpu.SemaphoreType.DMA((2, blocks)),
+        ),
+    )
     key_grad, value_grad = call(
         finish_kernel, "finish",
         (Far(shape(token_shape, bf16)), Far(shape(token_shape, bf16))),
-        (Held(keys), Held(values), leaving, table, Held(key_part), Far(value_part)),
+        (Held(keys), Held(values), leaving, table, Far(key_part), Far(value_part)),
         scratch=(
-            pltpu.VMEM(token_shape, f32),
-            pltpu.VMEM(token_shape, bf16),
-            pltpu.VMEM(token_shape, bf16),
-            pltpu.SemaphoreType.DMA((tokens // block_rows,)),
-            pltpu.SemaphoreType.DMA((2 * tokens // block_rows,)),
+            wide, wide, narrow, narrow,
+            pltpu.SemaphoreType.DMA((2, blocks)),
+            pltpu.SemaphoreType.DMA((2, blocks)),
         ),
     )
     return output, query_grad, key_grad, value_grad, gain_sum.reshape(channels)

time: 117 us -> 114 us (0.974)
  blocking collectives: 56.8 us -> 34.2 us
  waiting for transfers between devices: 13.6 us -> 24.9 us
  Pallas kernels: 19.5 us -> 26.6 us
  starting transfers between devices: 19.8 us -> 25.1 us
  local copies, waits for them, and re-layouts: 5.93 us -> 1.36 us
    all_to_all x2 -> x1, blocking collectives: 40.8 us -> 18.1 us  [exchange(): return lax.all_to_all(flat, 'seq', 0, 0, tiled=True).reshape(pieces.shape)]
    all_to_all x2 -> x3, waiting for transfers between devices: 13.6 us -> 24.9 us  [exchange(): return lax.all_to_all(flat, 'seq', 0, 0, tiled=True).reshape(pieces.shape)]
    pallas_call x8 -> x9, Pallas kernels: 19.5 us -> 26.6 us  [call(): pl.pallas_call(kernel, out_shape=tuple((bare(x) for x in out_shape)), in_...]
    all_to_all x2 -> x3, starting transfers between devices: 19.8 us -> 25.1 us  [exchange(): return lax.all_to_all(flat, 'seq', 0, 0, tiled=True).reshape(pieces.shape)]
    unnamed x28 -> x20, local copies, waits for them, and re-layouts: 5.93 us -> 1.36 us
  transfers between devices with their start and end apart: 2 -> 3, of which waited for: 2 -> 3; matrix products, arithmetic and copies ran while one was open for 0% -> 0% of each run, Pallas kernels for 9% -> 15%
where the time goes in v3:
time: 114 us; the launch traced here: 113 us
  blocking collectives  34.2 us (30%)
  Pallas kernels  26.6 us (23%)
  starting transfers between devices  25.1 us (22%)
  waiting for transfers between devices  24.9 us (22%)
  local copies, waits for them, and re-layouts  1.36 us (1%)
    pallas_call x9, Pallas kernels, call(): pl.pallas_call(kernel, out_shape=tuple((bare(x) for x in out_shape)), in_...  26.6 us
    all_to_all x3, starting transfers between devices, exchange(): return lax.all_to_all(flat, 'seq', 0, 0, tiled=True).reshape(pieces.shape)  25.1 us
    all_to_all x3, waiting for transfers between devices, exchange(): return lax.all_to_all(flat, 'seq', 0, 0, tiled=True).reshape(pieces.shape)  24.9 us
    all_to_all x1, blocking collectives, exchange(): return lax.all_to_all(flat, 'seq', 0, 0, tiled=True).reshape(pieces.shape)  18.1 us
    all_to_all x1, blocking collectives, local(): sums = Held(lax.all_to_all(sums, 'head', 0, 0, tiled=True))  16 us
  transfers between devices with their start and end apart: 3, of which 3 were waited for; matrix products, arithmetic and copies ran while one was open for 0% of the time, Pallas kernels for 15%

profile of v3, /device:TPU:32, one launch (start us, length us, event | category | flops | bytes accessed | tf_op | source)
XLA Modules:
  0.0 113.1 jit_solution(18019071153936973755)
XLA Ops:
  0.6 2.6 %own_state.1 = (f32[272,128]{1,0:T(8,128)}, f32[256,128]{1,0:T(8,128)S(1)}, f32[8,256]{1,0:T(8,128)S(1)}) custom-call(f32[2,1024]{1,0:T(2,128)} %far_decay_ref.1, bf16[1024,256]{1,0:T(8,128)(2,1)} %keys_ref.1, bf16[1024,256]{1,0:T(8,128)(2,1)} %values_ref.1), custom_call_target="tpu_custom_call" | custom-call | bytes 1048576 | tf_op jit(solution)/shard_map/own_state/pallas_call | solution.py:537
  3.2 0.0 copy-start.6
  3.2 15.2 %all-to-all-start = ((f32[16,1,2176]{2,1,0:T(1,128)}), f32[16,1,2176]{2,1,0:T(1,128)S(1)}, u32[]{:S(2)}, u32[]{:S(2)}) async-start(f32[16,1,2176]{2,1,0:T(1,128)} %bitcast.1), calls=%async_computation | async-start | bytes 278528 | tf_op jit(solution)/shard_map/scan_out/all_to_all | solution.py:513
  18.5 0.0 copy-start.9
  18.5 0.0 copy-done.6
  18.5 0.7 copy-done.9
  19.1 0.0 copy-start.4
  19.2 3.8 %inside.1 = (f32[1024,256]{1,0:T(8,128)S(1)}, f32[1,256]{1,0:T(1,128)S(1)}, f32[8,128]{1,0:T(8,128)S(1)}) custom-call(bf16[1024,256]{1,0:T(8,128)(2,1)} %far_queries_ref.3, bf16[1024,256]{1,0:T(8,128)(2,1)} %keys_ref.1, bf16[1024,256]{1,0:T(8,128)(2,1)} %values_ref.1, f32[256,128]{1,0:T(8,128)S(1)} %get-tuple-element.25.table_ref.refs_5_, ...), custom_call_target="tpu_custom_call" | custom-call | flops 536870912 | bytes 1048576 | tf_op jit(solution)/shard_map/inside/pallas_call | solution.py:537
  23.0 0.0 copy-start.3
  23.0 9.9 %all-to-all-done = f32[16,1,2176]{2,1,0:T(1,128)S(1)} async-done(((f32[16,1,2176]{2,1,0:T(1,128)}), f32[16,1,2176]{2,1,0:T(1,128)S(1)}, u32[]{:S(2)}, u32[]{:S(2)}) %all-to-all-start) | async-done | bytes 139296 | tf_op jit(solution)/shard_map/scan_out/all_to_all | solution.py:513
  32.9 18.1 %all_to_all.25 = f32[16,1,2048]{2,1,0:T(1,128)S(1)} all-to-all(f32[16,1,2048]{2,1,0:T(1,128)S(1)} %bitcast.15), channel_id=1, replica_groups=mesh['seq'=16,'head'=32] {'seq'}, dimensions={0} | all-to-all | bytes 262144 | tf_op jit(solution)/shard_map/scan_back/all_to_all | solution.py:513
  51.0 0.0 copy-done.4
  51.0 0.0 copy-done.3
  51.0 1.0 attend.1
  52.0 0.0 copy-start.2
  52.0 16.0 %all_to_all.26.refs_0_ = f32[32,16,128]{2,1,0:T(8,128)S(1)} all-to-all(f32[32,16,128]{2,1,0:T(8,128)S(1)} %get-tuple-element.32), channel_id=1, replica_groups=mesh['seq'=16,'head'=32] {'head'}, dimensions={0} | all-to-all | bytes 524288 | tf_op jit(solution)/shard_map/head_sums/all_to_all | solution.py:602
  68.1 2.5 %norm_grad.1 = (f32[1024,256]{1,0:T(8,128)}, f32[128,128]{1,0:T(8,128)}, f32[288,128]{1,0:T(8,128)}) custom-call(f32[32,16,128]{2,1,0:T(8,128)S(1)} %all_to_all.26.refs_0_, f32[1024,256]{1,0:T(8,128)S(1)} %get-tuple-element.31.refs_1_.far_attended_ref, bf16[1024,256]{1,0:T(8,128)(2,1)S(1)} %copy-done.3, f32[1,256]{1,0:T(1,128)S(1)} %get-tuple-element.27.gain_ref.refs_3_, ...), custom_call_target="tpu_custom_call" | custom-call | bytes 1048576 | tf_op jit(solution)/shard_map/norm_grad/pallas_call | solution.py:537
  70.6 0.0 copy-done.2
  70.6 0.0 copy-start.7
  70.6 4.4 %all-to-all-start.3 = ((f32[16,1,2304]{2,1,0:T(1,128)}), f32[16,1,2304]{2,1,0:T(1,128)S(1)}, u32[]{:S(2)}, u32[]{:S(2)}) async-start(f32[16,1,2304]{2,1,0:T(1,128)} %bitcast.5), calls=%async_computation.3 | async-start | bytes 294912 | tf_op jit(solution)/shard_map/back_out/all_to_all | solution.py:513
  75.0 0.0 copy-done.7
  75.0 7.8 %key_value.1 = (f32[1024,256]{1,0:T(8,128)}, f32[1024,256]{1,0:T(8,128)}, f32[8,128]{1,0:T(8,128)S(1)}) custom-call(bf16[1024,256]{1,0:T(8,128)(2,1)} %far_queries_ref.3, bf16[1024,256]{1,0:T(8,128)(2,1)} %keys_ref.1, bf16[1024,256]{1,0:T(8,128)(2,1)} %values_ref.1, f32[1024,256]{1,0:T(8,128)} %get-tuple-element.33.far_grad_ref, ...), custom_call_target="tpu_custom_call" | custom-call | flops 1207959552 | bytes 1048576 | tf_op jit(solution)/shard_map/key_value/pallas_call | solution.py:537
  82.8 6.8 %all-to-all-done.3 = f32[16,1,2304]{2,1,0:T(1,128)S(1)} async-done(((f32[16,1,2304]{2,1,0:T(1,128)}), f32[16,1,2304]{2,1,0:T(1,128)S(1)}, u32[]{:S(2)}, u32[]{:S(2)}) %all-to-all-start.3) | async-done | bytes 147488 | tf_op jit(solution)/shard_map/back_out/all_to_all | solution.py:513
  89.6 0.7 suffix.1
  90.3 5.4 %all-to-all-start.4 = ((f32[16,1,2048]{2,1,0:T(1,128)}), f32[16,1,2048]{2,1,0:T(1,128)S(1)}, u32[]{:S(2)}, u32[]{:S(2)}) async-start(f32[16,1,2048]{2,1,0:T(1,128)} %bitcast.7), calls=%async_computation.4 | async-start | bytes 262144 | tf_op jit(solution)/shard_map/back_back/all_to_all | solution.py:513
  95.7 0.0 copy-done.5
  95.7 0.7 copy-done.8
  96.4 5.2 %query_grad.1 = (bf16[1024,256]{1,0:T(8,128)(2,1)}, bf16[1024,256]{1,0:T(8,128)(2,1)}) custom-call(f32[1024,256]{1,0:T(8,128)} %copy-done.2, f32[1024,256]{1,0:T(8,128)} %get-tuple-element.33.far_grad_ref, bf16[1024,256]{1,0:T(8,128)(2,1)} %keys_ref.1, bf16[1024,256]{1,0:T(8,128)(2,1)} %values_ref.1, f32[1,256]{1,0:T(1,128)S(1)} %get-tuple-element.27.gain_ref.refs_3_, ...), custom_call_target="tpu_custom_call" | custom-call | flops 939524096 | bytes 1048576 | tf_op jit(solution)/shard_map/query_grad/pallas_call | solution.py:537
  101.6 8.3 %all-to-all-done.4 = f32[16,1,2048]{2,1,0:T(1,128)S(1)} async-done(((f32[16,1,2048]{2,1,0:T(1,128)}), f32[16,1,2048]{2,1,0:T(1,128)S(1)}, u32[]{:S(2)}, u32[]{:S(2)}) %all-to-all-start.4) | async-done | bytes 131104 | tf_op jit(solution)/shard_map/back_back/all_to_all | solution.py:513
  109.8 0.0 copy-done
  109.8 0.0 copy-done.1
  109.8 3.1 %finish.1 = (bf16[1024,256]{1,0:T(8,128)(2,1)}, bf16[1024,256]{1,0:T(8,128)(2,1)}) custom-call(bf16[1024,256]{1,0:T(8,128)(2,1)S(1)} %copy-done, bf16[1024,256]{1,0:T(8,128)(2,1)S(1)} %copy-done.1, f32[256,128]{1,0:T(8,128)S(1)} %bitcast.16, f32[256,128]{1,0:T(8,128)S(1)} %get-tuple-element.25.table_ref.refs_5_, ...), custom_call_target="tpu_custom_call" | custom-call | bytes 1048576 | tf_op jit(solution)/shard_map/finish/pallas_call | solution.py:537
  (5 shorter events, 0.0 us)
Async XLA Ops:
  3.2 15.2 %copy-start.6 = (f32[8,256]{1,0:T(8,128)}, f32[8,256]{1,0:T(8,128)S(1)}, u32[]{:S(2)}) copy-start(f32[8,256]{1,0:T(8,128)S(1)} %get-tuple-element.26.rows_ref) | copy-start | bytes 24580
  3.2 29.6 %all-to-all-start = ((f32[16,1,2176]{2,1,0:T(1,128)}), f32[16,1,2176]{2,1,0:T(1,128)S(1)}, u32[]{:S(2)}, u32[]{:S(2)}) async-start(f32[16,1,2176]{2,1,0:T(1,128)} %bitcast.1), calls=%async_computation | async-start | bytes 278528 | tf_op jit(solution)/shard_map/scan_out/all_to_all | solution.py:513
  18.5 0.7 copy-start.9
  19.1 31.9 %copy-start.4 = (bf16[1024,256]{1,0:T(8,128)(2,1)S(1)}, bf16[1024,256]{1,0:T(8,128)(2,1)}, u32[]{:S(2)}) copy-start(bf16[1024,256]{1,0:T(8,128)(2,1)} %far_queries_ref.3) | copy-start | bytes 1572868
  23.0 28.0 %copy-start.3 = (bf16[1024,256]{1,0:T(8,128)(2,1)S(1)}, bf16[1024,256]{1,0:T(8,128)(2,1)}, u32[]{:S(2)}) copy-start(bf16[1024,256]{1,0:T(8,128)(2,1)} %refs_2_.1) | copy-start | bytes 1572868
  52.0 18.6 %copy-start.2 = (f32[1024,256]{1,0:T(8,128)}, f32[1024,256]{1,0:T(8,128)S(1)}, u32[]{:S(2)}) copy-start(f32[1024,256]{1,0:T(8,128)S(1)} %get-tuple-element.31.refs_1_.far_attended_ref) | copy-start | bytes 3145732
  70.6 4.4 %copy-start.7 = (f32[8,256]{1,0:T(8,128)S(1)}, f32[8,256]{1,0:T(8,128)}, u32[]{:S(2)}) copy-start(f32[8,256]{1,0:T(8,128)} %copy-done.6) | copy-start | bytes 24580
  70.6 19.0 %all-to-all-start.3 = ((f32[16,1,2304]{2,1,0:T(1,128)}), f32[16,1,2304]{2,1,0:T(1,128)S(1)}, u32[]{:S(2)}, u32[]{:S(2)}) async-start(f32[16,1,2304]{2,1,0:T(1,128)} %bitcast.5), calls=%async_computation.3 | async-start | bytes 294912 | tf_op jit(solution)/shard_map/back_out/all_to_all | solution.py:513
  90.3 5.4 %copy-start.5 = (f32[128,128]{1,0:T(8,128)S(1)}, f32[128,128]{1,0:T(8,128)}, u32[]{:S(2)}) copy-start(f32[128,128]{1,0:T(8,128)} %get-tuple-element.34.scales_ref) | copy-start | bytes 196612
  90.3 19.5 %all-to-all-start.4 = ((f32[16,1,2048]{2,1,0:T(1,128)}), f32[16,1,2048]{2,1,0:T(1,128)S(1)}, u32[]{:S(2)}, u32[]{:S(2)}) async-start(f32[16,1,2048]{2,1,0:T(1,128)} %bitcast.7), calls=%async_computation.4 | async-start | bytes 262144 | tf_op jit(solution)/shard_map/back_back/all_to_all | solution.py:513
  95.7 0.7 copy-start.8
  96.4 13.5 %copy-start = (bf16[1024,256]{1,0:T(8,128)(2,1)S(1)}, bf16[1024,256]{1,0:T(8,128)(2,1)}, u32[]{:S(2)}) copy-start(bf16[1024,256]{1,0:T(8,128)(2,1)} %keys_ref.1) | copy-start | bytes 1572868
  96.4 13.5 %copy-start.1 = (bf16[1024,256]{1,0:T(8,128)(2,1)S(1)}, bf16[1024,256]{1,0:T(8,128)(2,1)}, u32[]{:S(2)}) copy-start(bf16[1024,256]{1,0:T(8,128)(2,1)} %values_ref.1) | copy-start | bytes 1572868
